TPU v7x, 32 devices: a whole 2x2x4 slice. The times are simulated.
32 devices in a mesh: side: 2 (over x), row: 4 (over z), col: 4 (over y, core).
Axes of the slice: x: 2, y: 2, z: 4, core: 2. Of those that a mesh axis runs over, the one named last changes fastest.
Arguments:
- old_vectors: bfloat16 [2, 32768, 16384], P('side', 'row', 'col'), may hold values from -6 to 6
- reflectors: bfloat16 [2, 2, 32768, 512], P('side', None, 'row', 'col'), may hold values from -0.0625 to 0.0625
- triangles: float32 [2, 2, 512, 512], P('side'), may hold values from -0.25 to 0.25
- pole_sq: float32 [32768], replicated, may hold values from 1 to 65536, as said below
- coupling: float32 [32768], replicated, may hold values from -1 to 1
- deflated: int32 [32768], replicated, may hold values 0 or 1
- pole_order: int32 [32768], replicated, may hold values from 0 to 32767, each once
- anchors: int32 [1024], replicated, may hold values from 0 to 32766, as said below
- root_fraction: float32 [1024], replicated, may hold values from 0.2 to 0.8
Outputs:
- vectors: bfloat16 [2, 1024, 32768], P('side', 'col', 'row')
Inputs may be any that keep to these rules, and one draw needn't show every extreme that they name: `pole_sq`: strictly increasing; successive entries differ by 0.5 or more. `anchors`: distinct entries.
All inputs are finite; a program needn't handle non-finite values.
Results may differ from a plain program's by a relative error of at most 0.014.
Values may be sent and summed in bfloat16 or wider, within the bound.
No kernel may reach another device: no remote copies, remote signals or barrier semaphores. Data moves between devices by JAX's collectives and lax.ppermute only.
A program may use at most 192 MiB of HBM per device.

v0:
```python
import jax
import jax.numpy as jnp
from jax import lax
from jax.sharding import PartitionSpec as P


def secular_columns(col_sq, col_coupling, col_live, weight, anchor_sq, pole_gap, root_fraction):
    denom = col_sq[:, None] - anchor_sq[None, :] - root_fraction[None, :] * pole_gap[None, :]
    return (col_live * col_coupling * weight)[:, None] / denom


def per_device(
    old_vectors,
    reflectors,
    triangles,
    pole_sq,
    coupling,
    deflated,
    pole_order,
    anchors,
    root_fraction,
):
    side_index = lax.axis_index("side")
    row_index = lax.axis_index("row")
    col_index = lax.axis_index("col")
    half_rows = lax.axis_size("row") // 2
    col_count = lax.axis_size("col")
    old_block = old_vectors[0]
    col_width = old_block.shape[1]
    order_size = pole_sq.shape[0]
    triplets = anchors.shape[0]
    local_triplets = triplets // col_count
    first_column = row_index // half_rows * (order_size // 2) + col_index * col_width
    columns = first_column + jnp.arange(col_width, dtype=jnp.int32)
    position = (
        jnp.zeros((order_size,), jnp.int32)
        .at[pole_order]
        .set(jnp.arange(order_size, dtype=jnp.int32))
    )
    sorted_pos = lax.dynamic_slice_in_dim(position, first_column, col_width)
    col_sq = pole_sq[sorted_pos]
    col_coupling = coupling[sorted_pos]
    col_live = (1 - deflated[sorted_pos]).astype(jnp.float32)
    weight = jnp.where(side_index == 0, jnp.ones_like(col_sq), jnp.sqrt(col_sq))
    anchor_sq = pole_sq[anchors]
    pole_gap = pole_sq[anchors + 1] - anchor_sq
    dead_triplet = deflated[anchors] == 1
    target = pole_order[anchors]
    secular = secular_columns(
        col_sq, col_coupling, col_live, weight, anchor_sq, pole_gap, root_fraction
    )
    onehot = (columns[:, None] == target[None, :]).astype(jnp.float32)
    mixing = jnp.where(dead_triplet[None, :], onehot, secular).astype(jnp.bfloat16)
    share_size = col_width // half_rows
    slice_part = lax.dynamic_slice_in_dim(
        secular, row_index % half_rows * share_size, share_size, 0
    )
    squares = lax.psum(jnp.sum(slice_part * slice_part, axis=0), ("row", "col"))
    col_scale = jnp.where(dead_triplet, jnp.ones_like(squares), 1.0 / jnp.sqrt(squares + 1e-06))
    merged = lax.psum_scatter(
        jnp.einsum("ck,rc->kr", mixing, old_block, preferred_element_type=jnp.float32).astype(
            jnp.bfloat16
        ),
        "col",
        scatter_dimension=0,
        tiled=True,
    ).astype(jnp.float32)
    my_scale = lax.dynamic_slice_in_dim(col_scale, col_index * local_triplets, local_triplets)
    vectors = merged * my_scale[:, None]
    panel_local = reflectors[0]
    panels = panel_local.shape[0]
    upper_tri = jnp.triu(triangles[0])
    highest = lax.Precision.HIGHEST
    gathered = lax.all_gather(panel_local, "col", axis=2, tiled=True)
    vectors_low = vectors.astype(jnp.bfloat16)
    raw_proj = jnp.stack(
        [
            jnp.dot(vectors_low, gathered[index], preferred_element_type=jnp.float32)
            for index in range(panels)
        ]
    )
    pair_list = [(later, earlier) for later in range(panels) for earlier in range(later)]
    gram_blocks = jnp.stack(
        [
            jnp.dot(gathered[later].T, gathered[earlier], preferred_element_type=jnp.float32)
            for later, earlier in pair_list
        ]
    )
    raw_proj, gram_blocks = (
        lax.psum(raw_proj.astype(jnp.bfloat16), "row").astype(jnp.float32),
        lax.psum(gram_blocks.astype(jnp.bfloat16), "row").astype(jnp.float32),
    )
    coef_list = [None] * panels
    for panel_index in reversed(range(panels)):
        projected = raw_proj[panel_index]
        for later in range(panel_index + 1, panels):
            gram_pos = pair_list.index((later, panel_index))
            projected = projected - jnp.dot(
                coef_list[later].astype(jnp.float32), gram_blocks[gram_pos], precision=highest
            )
        coef_list[panel_index] = jnp.dot(
            projected, upper_tri[panel_index].T, precision=highest
        ).astype(jnp.bfloat16)
    for panel_index in reversed(range(panels)):
        vectors = vectors - jnp.dot(
            coef_list[panel_index], gathered[panel_index].T, preferred_element_type=jnp.float32
        )
    return vectors.astype(jnp.bfloat16)[None]


def solution(mesh):
    in_specs = (
        P("side", "row", "col"),
        P("side", None, "row", "col"),
        P("side", None, None, None),
        P(),
        P(),
        P(),
        P(),
        P(),
        P(),
    )
    out_specs = P("side", "col", "row")
    return jax.shard_map(
        per_device, mesh=mesh, in_specs=in_specs, out_specs=out_specs, check_vma=False
    )
```

profile of v0, /device:TPU:0, one launch (start us, length us, event | category | flops | bytes accessed | tf_op | source)
XLA Modules:
  0.0 562.3 jit_solution(9312000785382595250)
XLA Ops:
  6.5 0.0 copy-start
  6.5 0.0 copy-start.2
  6.5 0.0 all-gather.3.cloned.1.call-start
  6.5 0.7 all-gather.3.cloned.1.call-update
  7.3 0.0 reduce-scatter.2.cloned.1.call-start
  7.3 0.9 compare_select_fusion
  8.3 120.1 %scatter_custom_fusion = s32[32768]{0:T(1024)S(1)} fusion(s32[32768]{0:T(1024)S(1)} %compare_select_fusion, s32[32768]{0:T(1024)S(1)} %iota.24, s32[]{:T(128)} %constant.23.clone.1), kind=kCustom, calls=%fused_computation.44 | custom fusion | bytes 131076 | tf_op jit(solution)/shard_map/scatter | solution.py:38
  128.4 0.0 copy-done.2
  128.4 23.0 %gather_fusion.2 = s32[4096]{0:T(1024)S(1)} fusion(s32[32768]{0:T(1024)S(1)} %copy-done.2, s32[4096]{0:T(1024)S(1)} %fusion.31), kind=kCustom, calls=%fused_computation.2 | custom fusion | bytes 49152 | tf_op jit(solution)/shard_map/gather | solution.py:43
  151.4 0.0 copy-done
  151.5 0.0 copy-start.6
  151.5 23.0 %gather_fusion.4 = f32[4096]{0:T(1024)S(1)} fusion(f32[32768]{0:T(1024)S(1)} %copy-done, s32[4096]{0:T(1024)S(1)} %fusion.31), kind=kCustom, calls=%fused_computation.4 | custom fusion | bytes 49152 | tf_op jit(solution)/shard_map/gather | solution.py:41
  174.5 0.0 copy-done.6
  174.5 0.0 copy-start.4
  174.5 0.0 copy-start.3
  174.6 6.2 %gather_fusion.5 = f32[1024]{0:T(1024)S(1)} fusion(f32[32768]{0:T(1024)S(1)} %copy-done, s32[1024]{0:T(1024)S(1)} %get-tuple-element.10), kind=kCustom, calls=%fused_computation.5 | custom fusion | bytes 12288 | tf_op jit(solution)/shard_map/gather | solution.py:45
  180.7 6.2 %gather_fusion = s32[1024]{0:T(1024)S(1)} fusion(s32[32768]{0:T(1024)S(1)} %copy-done.2, s32[1024]{0:T(1024)S(1)} %get-tuple-element.10), kind=kCustom, calls=%fused_computation | custom fusion | bytes 12288 | tf_op jit(solution)/shard_map/gather | solution.py:47
  186.9 0.0 copy-done.4
  186.9 6.2 %gather_fusion.1 = s32[1024]{0:T(1024)S(1)} fusion(s32[32768]{0:T(1024)S(1)} %copy-done.4, s32[1024]{0:T(1024)S(1)} %get-tuple-element.10), kind=kCustom, calls=%fused_computation.1 | custom fusion | bytes 12288 | tf_op jit(solution)/shard_map/gather | solution.py:48
  193.1 0.0 copy-done.3
  193.1 0.0 copy-start.7
  193.1 23.0 %gather_fusion.3 = f32[4096]{0:T(1024)S(1)} fusion(f32[32768]{0:T(1024)S(1)} %copy-done.3, s32[4096]{0:T(1024)S(1)} %fusion.31), kind=kCustom, calls=%fused_computation.3 | custom fusion | bytes 49152 | tf_op jit(solution)/shard_map/gather | solution.py:42
  216.1 6.2 %gather_fusion.6 = f32[1024]{0:T(1024)S(1)} fusion(f32[32768]{0:T(1024)S(1)} %copy-done, s32[1024]{0:T(1024)S(1)} %get-tuple-element.9), kind=kCustom, calls=%fused_computation.6 | custom fusion | bytes 12288 | tf_op jit(solution)/shard_map/gather | solution.py:46
  222.3 0.0 copy-done.7
  222.3 2.6 subtract_divide_fusion
  224.9 0.7 multiply_reduce_fusion
  225.6 35.1 %psum.21 = f32[1024]{0:T(1024)S(1)} all-reduce(f32[1024]{0:T(1024)S(1)} %multiply_reduce_fusion), channel_id=1, replica_groups=mesh['side'=2,'row'=4,'col'=4] {'row','col'}, use_global_device_ids=true, to_apply=%region_3.4 | all-reduce | flops 1024 | bytes 8192 | tf_op jit(solution)/shard_map/psum | solution.py:58
  260.7 0.6 rsqrt_select_fusion
  261.3 7.7 %select_convert_fusion.4 = bf16[4096,1024]{1,0:T(8,128)(2,1)} fusion(s32[1024]{0:T(1024)S(1)} %gather_fusion.1, s32[4096]{0:T(1024)S(1)} %iota_add_fusion, pred[1024]{0:T(1024)(128)(4,1)S(1)} %get-tuple-element.8, f32[1024]{0:T(1024)S(1)} %subtract_multiply_fusion, f32[1024]{0:T(1024)S(1)} %gather_fusion.5, f32[4096]{0:T(1024)S(1)} %gather_fusion.4, ...), kind=kLoop, calls=%fused_computation.10.clone.clone.1 | loop fusion | flops 29360128 | bytes 8451072 | tf_op jit(solution)/shard_map/ck,rc->kr/dot_general | solution.py:61
  269.0 78.1 %fusion.2 = bf16[1024,8192]{1,0:T(8,128)(2,1)} fusion(bf16[1,8192,4096]{2,1,0:T(8,128)(2,1)} %param.9, bf16[4096,1024]{1,0:T(8,128)(2,1)} %select_convert_fusion.4), kind=kOutput, calls=%fused_computation.12 | convolution fusion | flops 68727865344 | bytes 92274688 | tf_op jit(solution)/shard_map/ck,rc->kr/dot_general | solution.py:61
  347.1 0.0 reduce-scatter.2.cloned.1.call-update
  347.1 0.3 all-reduce.3.cloned.1.call-start
  347.4 0.8 dynamic_slice.11
  348.1 0.0 all-gather.3.cloned.1.call-done
  348.1 13.8 %fusion.16 = bf16[512,512]{1,0:T(8,128)(2,1)} fusion(bf16[1,2,8192,512]{3,2,1,0:T(8,128)(2,1)} %all-gather.3.cloned.1.call-done), kind=kOutput, calls=%fused_computation.29 | convolution fusion | flops 4295229440 | bytes 17301504 | tf_op jit(solution)/shard_map/dot_general | solution.py:85
  362.0 107.6 %reduce-scatter.2.cloned.1.call-done = bf16[256,8192]{1,0:T(8,128)(2,1)} async-done(((bf16[1024,8192]{1,0:T(8,128)(2,1)}), bf16[256,8192]{1,0:T(8,128)(2,1)}) %reduce-scatter.2.cloned.1.call-update) | async-done | bytes 4194320 | tf_op jit(solution)/shard_map/reduce_scatter | solution.py:60
  469.6 0.0 copy-start.5
  469.6 7.1 %fusion.23 = bf16[1,256,512]{2,1,0:T(8,128)(2,1)S(1)} fusion(bf16[1,2,8192,512]{3,2,1,0:T(8,128)(2,1)} %all-gather.3.cloned.1.call-done, bf16[256,8192]{1,0:T(8,128)(2,1)} %reduce-scatter.2.cloned.1.call-done, f32[256]{0:T(256)S(1)} %dynamic_slice.11), kind=kOutput, calls=%fused_computation.35 | convolution fusion | flops 2153906176 | bytes 12846080 | tf_op jit(solution)/shard_map/dot_general | solution.py:78
  476.7 2.3 copy-done.5
  479.0 4.6 fusion.26
  483.6 0.8 pad_maximum_fusion
  484.4 0.0 all-reduce.3.cloned.1.call-update
  484.4 0.2 iota_compare_fusion
  484.7 2.0 bitcast_select_fusion
  486.6 49.9 %all-reduce.3.cloned.1.call-done = (bf16[2,256,512]{2,1,0:T(8,128)(2,1)}, bf16[512,512]{1,0:T(8,128)(2,1)}) async-done(((bf16[2,256,512]{2,1,0:T(8,128)(2,1)}, bf16[512,512]{1,0:T(8,128)(2,1)}), (bf16[2,256,512]{2,1,0:T(8,128)(2,1)}, bf16[512,512]{1,0:T(8,128)(2,1)})) %all-reduce.3.cloned.1.call-update) | async-done | bytes 1048592 | tf_op jit(solution)/shard_map/psum | solution.py:90
  536.5 1.6 convolution_convert_fusion.1
  538.2 1.4 convolution_subtract_fusion.2
  539.6 1.1 convolution_convert_fusion
  540.6 0.0 copy-start.1
  540.7 7.1 %convolution_subtract_fusion.1 = f32[256,8192]{1,0:T(8,128)S(1)} fusion(bf16[256,512]{1,0:T(8,128)(2,1)S(1)} %convolution_convert_fusion.1, bf16[256,8192]{1,0:T(8,128)(2,1)} %reduce-scatter.2.cloned.1.call-done, bf16[1,2,8192,512]{3,2,1,0:T(8,128)(2,1)} %all-gather.3.cloned.1.call-done, f32[256]{0:T(256)S(1)} %dynamic_slice.11), kind=kOutput, calls=%fused_computation.14 | convolution fusion | flops 2153775104 | bytes 21234688 | tf_op jit(solution)/shard_map/dot_general | solution.py:105
  547.8 8.0 %fusion.6 = bf16[1,256,8192]{2,1,0:T(8,128)(2,1)} fusion(f32[256,8192]{1,0:T(8,128)S(1)} %convolution_subtract_fusion.1, bf16[256,512]{1,0:T(8,128)(2,1)S(1)} %convolution_convert_fusion, bf16[1,2,8192,512]{3,2,1,0:T(8,128)(2,1)} %all-gather.3.cloned.1.call-done), kind=kOutput, calls=%fused_computation.16 | convolution fusion | flops 2151677952 | bytes 21233664 | tf_op jit(solution)/shard_map/dot_general | solution.py:105
  555.8 0.0 copy-done.1
  (7 shorter events, 0.1 us)
Async XLA Ops:
  6.5 144.9 %copy-start = (f32[32768]{0:T(1024)S(1)}, f32[32768]{0:T(1024)}, u32[]{:S(2)}) copy-start(f32[32768]{0:T(1024)} %param.12) | copy-start | bytes 393220
  6.5 121.9 %copy-start.2 = (s32[32768]{0:T(1024)S(1)}, s32[32768]{0:T(1024)}, u32[]{:S(2)}) copy-start(s32[32768]{0:T(1024)} %param.14) | copy-start | bytes 393220
  6.5 341.6 %all-gather.3.cloned.1.call-start = ((), (), s32[]{:S(2)}) async-start(), calls=%async_computation.2 | async-start | bytes 20971520 | tf_op jit(solution)/shard_map/all_gather | solution.py:74
  7.3 462.3 %reduce-scatter.2.cloned.1.call-start = ((), (), s32[]{:S(2)}) async-start(), calls=%async_computation.1 | async-start | bytes 20971520 | tf_op jit(solution)/shard_map/reduce_scatter | solution.py:60
  151.5 23.1 %copy-start.6 = (s32[1024]{0:T(1024)S(1)}, s32[1024]{0:T(1024)}, u32[]{:S(2)}) copy-start(s32[1024]{0:T(1024)} %param.16) | copy-start | bytes 12292
  174.5 12.4 %copy-start.4 = (s32[32768]{0:T(1024)S(1)}, s32[32768]{0:T(1024)}, u32[]{:S(2)}) copy-start(s32[32768]{0:T(1024)} %param.15) | copy-start | bytes 393220
  174.5 18.5 %copy-start.3 = (f32[32768]{0:T(1024)S(1)}, f32[32768]{0:T(1024)}, u32[]{:S(2)}) copy-start(f32[32768]{0:T(1024)} %param.13) | copy-start | bytes 393220
  193.1 29.2 %copy-start.7 = (f32[1024]{0:T(1024)S(1)}, f32[1024]{0:T(1024)}, u32[]{:S(2)}) copy-start(f32[1024]{0:T(1024)} %param.17) | copy-start | bytes 12292
  347.1 189.4 %all-reduce.3.cloned.1.call-start = ((), (), s32[]{:S(2)}) async-start(), calls=%async_computation.3 | async-start | bytes 2097152 | tf_op jit(solution)/shard_map/psum | solution.py:90
  469.6 9.4 %copy-start.5 = (bf16[1,2,8192,512]{3,2,1,0:T(8,128)(2,1)S(1)}, bf16[1,2,8192,512]{3,2,1,0:T(8,128)(2,1)}, u32[]{:S(2)}) copy-start(bf16[1,2,8192,512]{3,2,1,0:T(8,128)(2,1)} %all-gather.3.cloned.1.call-done) | copy-start | bytes 50331652
  540.6 15.1 %copy-start.1 = (f32[32768]{0:T(1024)S(1)}, f32[32768]{0:T(1024)}, u32[]{:S(2)}) copy-start(f32[32768]{0:T(1024)} %param.12) | copy-start | bytes 393220
Sparse Core Ops, SparseCore 0:
  8.9 110.8 all-gather.2
  347.2 122.2 reduce-scatter.1
  484.6 51.9 all-reduce.2
where the time goes:
time: 563 us; the launch traced here: 562 us
  local copies, waits for them, and re-layouts  217 us (39%)
  waiting for transfers between devices  158 us (28%)
  matrix products  123 us (22%)
  blocking collectives  35.1 us (6%)
  other arithmetic  15.5 us (3%)
  between operations  13.4 us (2%)
    scatter x1, local copies, waits for them, and re-layouts, per_device(): position = jnp.zeros((order_size,), jnp.int32).at[pole_order].set(jnp.ara...  120 us
    reduce_scatter x1, waiting for transfers between devices, per_device(): lax.psum_scatter(jnp.einsum('ck,rc->kr', mixing, old_block, preferred_ele...  108 us
    dot_general x1, matrix products, per_device(): jnp.einsum('ck,rc->kr', mixing, old_block, preferred_element_type=jnp.flo...  78.1 us
    psum x1, waiting for transfers between devices, per_device(): lax.psum(raw_proj.astype(jnp.bfloat16), 'row').astype(jnp.float32)  49.9 us
    psum x1, blocking collectives, per_device(): squares = lax.psum(jnp.sum(slice_part * slice_part, axis=0), ('row', 'col'))  35.1 us
    gather x1, local copies, waits for them, and re-layouts, per_device(): col_live = (1 - deflated[sorted_pos]).astype(jnp.float32)  23 us
    gather x1, local copies, waits for them, and re-layouts, per_device(): col_sq = pole_sq[sorted_pos]  23 us
    gather x1, local copies, waits for them, and re-layouts, per_device(): col_coupling = coupling[sorted_pos]  23 us
  transfers between devices with their start and end apart: 3, of which 2 were waited for; matrix products, arithmetic and copies ran while one was open for 57% of the time, Pallas kernels for 0%

commit v1 on v0

v1 whole, which is shorter than its diff:
```python
import jax
import jax.numpy as jnp
from jax import lax
from jax.experimental import pallas as pl
from jax.experimental.pallas import tpu as pltpu
from jax.sharding import PartitionSpec as P


LANES = 128
HIGHEST = lax.Precision.HIGHEST
NT = (((1,), (1,)), ((), ()))
TN = (((0,), (0,)), ((), ()))


def tile_of(size, want):
    tile = min(size, want)
    while size % tile:
        tile //= 2
    return tile


def split3(x):
    first = x.astype(jnp.bfloat16).astype(jnp.float32)
    rest = x - first
    second = rest.astype(jnp.bfloat16).astype(jnp.float32)
    return first, second, rest - second


def add_up(step, total_ref, value):
    @pl.when(step == 0)
    def _():
        total_ref[...] = value

    @pl.when(step > 0)
    def _():
        total_ref[...] += value


def column_kernel(place_ref, order_ref, sq_ref, coupling_ref, deflated_ref, out_sq_ref, out_num_ref, acc_ref):
    step = pl.program_id(0)

    rows = out_sq_ref.shape[0]
    chunk = order_ref.shape[1]
    local = order_ref[...] - place_ref[0]
    high = jnp.broadcast_to(local >> 7, (rows, chunk))
    low = jnp.broadcast_to(local & 127, (LANES, chunk))
    in_row = high == lax.broadcasted_iota(jnp.int32, (rows, chunk), 0)
    in_lane = jnp.where(low == lax.broadcasted_iota(jnp.int32, (LANES, chunk), 0), 1.0, 0.0)
    num = (1 - deflated_ref[...]).astype(jnp.float32) * coupling_ref[...]
    parts = [
        jnp.where(in_row, jnp.broadcast_to(part, (rows, chunk)), 0.0).astype(jnp.bfloat16)
        for part in split3(sq_ref[...]) + split3(num)
    ]
    add_up(
        step,
        acc_ref,
        lax.dot_general(
            jnp.concatenate(parts, axis=0),
            in_lane.astype(jnp.bfloat16),
            NT,
            preferred_element_type=jnp.float32,
        ),
    )

    @pl.when(step == pl.num_programs(0) - 1)
    def _():
        picked = [acc_ref[i * rows : (i + 1) * rows] for i in range(6)]
        col_sq = (picked[0] + picked[1]) + picked[2]
        weight = jnp.where(place_ref[1] == 0, jnp.ones_like(col_sq), jnp.sqrt(col_sq))
        out_sq_ref[...] = col_sq
        out_num_ref[...] = ((picked[3] + picked[4]) + picked[5]) * weight


def column_tables(place, pole_order, pole_sq, coupling, deflated, col_width):
    order_size = pole_order.shape[0]
    rows = col_width // LANES
    chunk = tile_of(order_size, 4096)
    row_spec = pl.BlockSpec((1, chunk), lambda i, place: (0, i))
    out_spec = pl.BlockSpec((rows, LANES), lambda i, place: (0, 0))
    return pl.pallas_call(
        column_kernel,
        grid_spec=pltpu.PrefetchScalarGridSpec(
            num_scalar_prefetch=1,
            grid=(order_size // chunk,),
            in_specs=[row_spec] * 4,
            out_specs=[out_spec] * 2,
            scratch_shapes=[pltpu.VMEM((6 * rows, LANES), jnp.float32)],
        ),
        out_shape=[jax.ShapeDtypeStruct((rows, LANES), jnp.float32)] * 2,
        name="columns",
    )(place, *(x.reshape(1, order_size) for x in (pole_order, pole_sq, coupling, deflated)))


def down(row, height=LANES):
    return jnp.broadcast_to(row, (height, row.shape[1])).T


def mixing_kernel(place_ref, anchors_ref, fraction_ref, pole_ref, deflated_ref, order_ref, sq_ref, num_ref,
                  mix_ref, squares_ref, dead_ref):
    count = anchors_ref.shape[2]
    anchor = anchors_ref[0]

    def lookup(index, tables):
        table_rows = tables.shape[0]
        onehot = jnp.where(
            lax.broadcasted_iota(jnp.int32, (table_rows, count), 0)
            == jnp.broadcast_to(index >> 7, (table_rows, count)),
            1.0,
            0.0,
        )
        found = lax.dot_general(tables, onehot, TN, precision=HIGHEST, preferred_element_type=jnp.float32)
        mask = lax.broadcasted_iota(jnp.int32, (LANES, count), 0) == jnp.broadcast_to(index & 127, (LANES, count))
        return [
            jnp.sum(jnp.where(mask, found[i : i + LANES], 0.0), axis=0, keepdims=True)
            for i in range(0, found.shape[0], LANES)
        ]

    poles = pole_ref[...]
    tables = jnp.concatenate(
        [poles, deflated_ref[...].astype(jnp.float32), order_ref[...].astype(jnp.float32)], axis=1
    )
    anchor_sq, dead, target = lookup(anchor, tables)
    (next_sq,) = lookup(anchor + 1, poles)
    dead_ref[0] = dead
    anchor_col = down(anchor_sq)
    shift_col = down(fraction_ref[0] * (next_sq - anchor_sq))
    dead_col = down(dead)
    target_col = down(target - place_ref[0].astype(jnp.float32))
    block = tile_of(count, 64)
    chunks = sq_ref.shape[0]
    sums = []
    for start in range(0, count, block):
        part = slice(start, start + block)
        base, shift = anchor_col[part], shift_col[part]
        is_dead, goal = dead_col[part] > 0.5, target_col[part]
        lane = lax.broadcasted_iota(jnp.int32, (block, LANES), 1).astype(jnp.float32)

        def body(c, total, part=part, base=base, shift=shift, is_dead=is_dead, goal=goal, lane=lane):
            col_sq = sq_ref[pl.ds(c, 1), :]
            den = (col_sq - base) - shift
            secular = num_ref[pl.ds(c, 1), :] / den
            first = c * LANES
            onehot = jnp.where(lane + first.astype(jnp.float32) == goal, 1.0, 0.0)
            mix_ref[part, pl.ds(pl.multiple_of(first, LANES), LANES)] = jnp.where(is_dead, onehot, secular).astype(
                jnp.bfloat16
            )
            return total + secular * secular

        sums.append(lax.fori_loop(0, chunks, body, jnp.zeros((block, LANES), jnp.float32), unroll=2))
    total = jnp.concatenate(sums, axis=0)
    squares_ref[0] = jnp.sum(total.T, axis=0, keepdims=True)


def mixing_rows(place, col_index, slots, anchors3, fraction3, tables, col_tables):
    count = anchors3.shape[2]
    rows = col_tables[0].shape[0]
    width = rows * LANES
    scalars = jnp.concatenate([place, jnp.asarray(slots, jnp.int32) ^ col_index])

    def pick(i, sc):
        return (sc[2 + i], 0, 0)

    row_spec = pl.BlockSpec((1, 1, count), pick)
    whole = lambda a: pl.BlockSpec(a.shape, lambda i, sc: (0,) * a.ndim)
    out_row = pl.BlockSpec((1, 1, count), lambda i, sc: (i, 0, 0))
    return pl.pallas_call(
        mixing_kernel,
        grid_spec=pltpu.PrefetchScalarGridSpec(
            num_scalar_prefetch=1,
            grid=(len(slots),),
            in_specs=[row_spec, row_spec] + [whole(t) for t in tables] + [whole(t) for t in col_tables],
            out_specs=[pl.BlockSpec((count, width), lambda i, sc: (i, 0)), out_row, out_row],
        ),
        out_shape=[
            jax.ShapeDtypeStruct((len(slots) * count, width), jnp.bfloat16),
            jax.ShapeDtypeStruct((len(slots), 1, count), jnp.float32),
            jax.ShapeDtypeStruct((len(slots), 1, count), jnp.float32),
        ],
        name="mixing",
    )(scalars, anchors3, fraction3, *tables, *col_tables)


def merge(mix, old, start, size, kept):
    total, depth = mix.shape
    rows = tile_of(size, 512)
    sent = total - kept[0] - kept[1]
    splits = [(0, sent), (sent, kept[0]), (sent + kept[0], kept[1])]
    first = start // rows

    def kernel(mix_ref, old_ref, *outs):
        value = lax.dot_general(mix_ref[...], old_ref[...], NT, preferred_element_type=jnp.float32)
        for (at, length), out in zip(splits, outs):
            out[...] = value[at : at + length].astype(jnp.bfloat16)

    return pl.pallas_call(
        kernel,
        grid=(size // rows,),
        in_specs=[
            pl.BlockSpec((total, depth), lambda i: (0, 0), pipeline_mode=pl.Buffered(1)),
            pl.BlockSpec((rows, depth), lambda i: (first + i, 0)),
        ],
        out_specs=[pl.BlockSpec((length, rows), lambda i: (0, i)) for _, length in splits],
        out_shape=[jax.ShapeDtypeStruct((length, size), jnp.bfloat16) for _, length in splits],
        name="merge",
    )(mix, old)


def ranges(parts, tile):
    found, at = [], 0
    for part in parts:
        found.append((at, part // tile))
        at += part // tile
    return found, at


def block_spec(height, tile, at, steps, row=0, lane=0):
    return pl.BlockSpec((height, tile), lambda i, sc: (row, lane + jnp.clip(i - at, 0, steps - 1)))


def project(place, parts, start, pieces, row_count, init=None, last=True):
    slots, (panels, _, wide) = len(pieces), pieces[0].shape
    count = parts[0][0].shape[0]
    order = slots * wide
    tile = tile_of(parts[0][0].shape[1], 1024)
    spans, steps = ranges([part[0].shape[1] for part in parts], tile)
    sub = count // row_count
    first = start // tile
    n_init = 0 if init is None else 1

    def kernel(sc_ref, *refs):
        part_refs, refs = refs[: 3 * len(parts)], refs[3 * len(parts) :]
        piece_refs, refs = refs[:slots], refs[slots:]
        init_refs, refs = refs[:n_init], refs[n_init:]
        outs, acc_ref = refs[:-1], refs[-1]
        step = pl.program_id(0)
        for n, (at, length) in enumerate(spans):
            far_ref, own_ref, sent_ref = part_refs[3 * n : 3 * n + 3]

            @pl.when((step >= at) & (step < at + length))
            def _(far_ref=far_ref, own_ref=own_ref, sent_ref=sent_ref):
                own = own_ref[...].astype(jnp.float32) + sent_ref[...].astype(jnp.float32)
                both = jnp.concatenate([far_ref[...], own.astype(jnp.bfloat16)], axis=0)
                for p in range(panels):
                    panel = jnp.concatenate([piece_refs[k][p] for k in range(slots)], axis=1)
                    value = jnp.dot(both, panel, preferred_element_type=jnp.float32)
                    if init is None:
                        add_up(step, acc_ref.at[p], value)
                    else:

                        @pl.when(step == 0)
                        def _(p=p, value=value):
                            acc_ref[p] = init_refs[0][p] + value

                        @pl.when(step > 0)
                        def _(p=p, value=value):
                            acc_ref[p] += value

        @pl.when(step == pl.num_programs(0) - 1)
        def _():
            if not last:
                outs[0][...] = acc_ref[...]
                return
            col, row = sc_ref[0], sc_ref[1]
            for t in range(row_count):
                at = pl.multiple_of((row ^ t) * sub, sub)
                for p in range(panels):
                    for k in range(slots):
                        lanes = pl.ds(pl.multiple_of(p * order + (col ^ k) * wide, wide), wide)
                        cols = slice(k * wide, (k + 1) * wide)
                        outs[0][t, :, lanes] = acc_ref[p, pl.ds(at, sub), cols].astype(jnp.bfloat16)
                        outs[1][t, :, lanes] = acc_ref[p, pl.ds(at + count, sub), cols].astype(jnp.bfloat16)

    acc_shape = (panels, 2 * count, order)
    if last:
        out_shapes = [jax.ShapeDtypeStruct((row_count, sub, panels * order), jnp.bfloat16)] * 2
    else:
        out_shapes = [jax.ShapeDtypeStruct(acc_shape, jnp.float32)]
    in_specs = []
    for at, length in spans:
        in_specs += [block_spec(count, tile, at, length)] * 2 + [block_spec(count, tile, at, length, row=1)]
    in_specs += [pl.BlockSpec((panels, tile, wide), lambda i, sc: (0, first + i, 0))] * slots
    if init is not None:
        in_specs += [pl.BlockSpec(acc_shape, lambda i, sc: (0, 0, 0), pipeline_mode=pl.Buffered(1))]
    return pl.pallas_call(
        kernel,
        grid_spec=pltpu.PrefetchScalarGridSpec(
            num_scalar_prefetch=1,
            grid=(steps,),
            in_specs=in_specs,
            out_specs=[pl.BlockSpec(s.shape, lambda i, sc: (0, 0, 0)) for s in out_shapes],
            scratch_shapes=[pltpu.VMEM(acc_shape, jnp.float32)],
        ),
        out_shape=out_shapes,
        name="project",
    )(place, *(a for part in parts for a in part), *pieces, *(() if init is None else (init,)))


def panel_products(place, pieces, row_count, pairs):
    slots, (panels, size, wide) = len(pieces), pieces[0].shape
    order = slots * wide
    tile = tile_of(size, 2048)
    sub_gram = order // row_count

    def kernel(sc_ref, *refs):
        piece_refs, (gram_out, gram_ref, nat_ref) = refs[:slots], refs[slots:]
        step = pl.program_id(0)
        for n, (later, earlier) in enumerate(pairs):
            panel = jnp.concatenate([piece_refs[k][later] for k in range(slots)], axis=1)
            product = lax.dot_general(
                panel, piece_refs[0][earlier], TN, preferred_element_type=jnp.float32
            )
            add_up(step, gram_ref.at[n], product)

        @pl.when(step == pl.num_programs(0) - 1)
        def _():
            col, row = sc_ref[0], sc_ref[1]
            for n in range(len(pairs)):
                for k in range(slots):
                    at = pl.multiple_of((col ^ k) * wide, wide)
                    nat_ref[pl.ds(at, wide), :] = gram_ref[n, k * wide : (k + 1) * wide, :]
                for t in range(row_count):
                    at = pl.multiple_of((row ^ t) * sub_gram, sub_gram)
                    gram_out[t, n] = nat_ref[pl.ds(at, sub_gram), :].astype(jnp.bfloat16)

    out_shape = jax.ShapeDtypeStruct((row_count, len(pairs), sub_gram, wide), jnp.bfloat16)
    return pl.pallas_call(
        kernel,
        grid_spec=pltpu.PrefetchScalarGridSpec(
            num_scalar_prefetch=1,
            grid=(size // tile,),
            in_specs=[pl.BlockSpec((panels, tile, wide), lambda i, sc: (0, i, 0))] * slots,
            out_specs=pl.BlockSpec(out_shape.shape, lambda i, sc: (0, 0, 0, 0)),
            scratch_shapes=[
                pltpu.VMEM((len(pairs), order, wide), jnp.float32),
                pltpu.VMEM((order, wide), jnp.float32),
            ],
        ),
        out_shape=out_shape,
        name="gram",
    )(place, *pieces)


def coefficients(place, shares, grams, triangles, pairs):
    panels, order = triangles.shape[0], triangles.shape[1]
    sub = shares[0].shape[0]
    slots = len(grams)
    row_count, _, sub_gram, wide = grams[0].shape

    def kernel(sc_ref, *refs):
        share_refs = refs[: len(shares)]
        gram_refs = refs[len(shares) : len(shares) + slots]
        tri_ref, out_ref, nat_ref = refs[len(shares) + slots :]
        col, row = sc_ref[0], sc_ref[1]
        for n in range(len(pairs)):
            for k in range(slots):
                for t in range(row_count):
                    rows = pl.ds(pl.multiple_of((row ^ t) * sub_gram, sub_gram), sub_gram)
                    lanes = pl.ds(pl.multiple_of((col ^ k) * wide, wide), wide)
                    nat_ref[n, rows, lanes] = gram_refs[k][t, n].astype(jnp.float32)
        total = share_refs[0][...].astype(jnp.float32)
        for ref in share_refs[1:]:
            total = total + ref[...].astype(jnp.float32)
        keep = lax.broadcasted_iota(jnp.int32, (order, order), 0) <= lax.broadcasted_iota(
            jnp.int32, (order, order), 1
        )
        found = [None] * panels
        for p in reversed(range(panels)):
            projected = total[:, p * order : (p + 1) * order]
            for later in range(p + 1, panels):
                gram = nat_ref[pairs.index((later, p))].astype(jnp.bfloat16)
                projected = projected - jnp.dot(found[later], gram, preferred_element_type=jnp.float32)
            upper = jnp.where(keep, tri_ref[p], 0.0)
            found[p] = lax.dot_general(
                projected, upper, NT, precision=HIGHEST, preferred_element_type=jnp.float32
            ).astype(jnp.bfloat16)
            out_ref[:, p * order : (p + 1) * order] = found[p]

    whole = lambda a: pl.BlockSpec(a.shape, lambda i, sc: (0,) * a.ndim)
    args = [*shares, *grams, triangles]
    return pl.pallas_call(
        kernel,
        grid_spec=pltpu.PrefetchScalarGridSpec(
            num_scalar_prefetch=1,
            grid=(1,),
            in_specs=[whole(a) for a in args],
            out_specs=pl.BlockSpec((sub, panels * order), lambda i, sc: (0, 0)),
            scratch_shapes=[pltpu.VMEM((len(pairs), order, order), jnp.float32)],
        ),
        out_shape=jax.ShapeDtypeStruct((sub, panels * order), jnp.bfloat16),
        name="coefficients",
    )(place, *args)


def finish(place, parts, start, pieces, coefs, scales, partial=None):
    slots, (panels, total_rows, wide) = len(pieces), pieces[0].shape
    count = parts[0][0].shape[0]
    order = slots * wide
    leads = partial is None
    tile = min([tile_of(part[2].shape[1], 1024) for part in parts])
    spans, steps = ranges([part[2].shape[1] for part in parts], tile)
    first = start // tile
    n_coef, n_scale = len(coefs), len(scales)

    def kernel(sc_ref, *refs):
        part_refs, refs = refs[: 3 * len(parts)], refs[3 * len(parts) :]
        piece_refs, refs = refs[:slots], refs[slots:]
        coef_refs, refs = refs[:n_coef], refs[n_coef:]
        scale_refs, refs = refs[:n_scale], refs[n_scale:]
        if leads:
            out_ref, coef_ref, scale_ref, wide_ref = refs
        else:
            out_ref, coef_ref, scale_ref = refs[1], coef_refs[0], scale_refs[0]
        step = pl.program_id(0)

        if leads:

            @pl.when(step == 0)
            def _():
                col, row = sc_ref[0], sc_ref[1]
                sub = coef_refs[0].shape[0]
                for t in range(n_coef):
                    rows = pl.ds(pl.multiple_of((row ^ t) * sub, sub), sub)
                    for p in range(panels):
                        for k in range(slots):
                            lanes = pl.ds(pl.multiple_of(p * order + (col ^ k) * wide, wide), wide)
                            at = p * order + k * wide
                            wide_ref[rows, at : at + wide] = coef_refs[t][:, lanes].astype(jnp.float32)
                coef_ref[...] = wide_ref[...].astype(jnp.bfloat16)
                squares = scale_refs[0][...] + scale_refs[1][...]
                scale = jnp.where(scale_refs[2][...] > 0.5, 1.0, 1.0 / jnp.sqrt(squares + 1e-06))
                scale_ref[...] = down(scale)

        for n, (at, length) in enumerate(spans):
            own_ref, sent_ref, arrived_ref = part_refs[3 * n : 3 * n + 3]

            @pl.when((step >= at) & (step < at + length))
            def _(own_ref=own_ref, sent_ref=sent_ref, arrived_ref=arrived_ref):
                total = own_ref[...].astype(jnp.float32) + sent_ref[...].astype(jnp.float32)
                total = total + arrived_ref[...].astype(jnp.float32)
                product = None
                for p in range(panels):
                    panel = jnp.concatenate([piece_refs[k][p] for k in range(slots)], axis=1)
                    value = lax.dot_general(
                        coef_ref[:, p * order : (p + 1) * order], panel, NT, preferred_element_type=jnp.float32
                    )
                    product = value if product is None else product + value
                scale = jnp.concatenate([scale_ref[...]] * (tile // LANES), axis=1)
                out_ref[...] = ((total - product) * scale).astype(jnp.bfloat16)

    whole = lambda a: pl.BlockSpec(a.shape, lambda i, sc: (0,) * a.ndim)
    in_specs, args = [], []
    for (own, sent, arrived, lane), (at, length) in zip(parts, spans):
        in_specs += [
            block_spec(count, tile, at, length, lane=lane // tile),
            block_spec(count, tile, at, length, row=1, lane=lane // tile),
            block_spec(count, tile, at, length),
        ]
        args += [own, sent, arrived]
    in_specs += [pl.BlockSpec((panels, tile, wide), lambda i, sc: (0, first + i, 0))] * slots
    in_specs += [whole(a) for a in (*coefs, *scales)]
    args += [*pieces, *coefs, *scales]
    out_specs = [pl.BlockSpec((count, tile), lambda i, sc: (0, first + i))]
    out_shape = [jax.ShapeDtypeStruct((count, total_rows), jnp.bfloat16)]
    scratch, aliases = [], {}
    if leads:
        out_specs += [
            pl.BlockSpec((count, panels * order), lambda i, sc: (0, 0)),
            pl.BlockSpec((count, LANES), lambda i, sc: (0, 0)),
        ]
        out_shape += [
            jax.ShapeDtypeStruct((count, panels * order), jnp.bfloat16),
            jax.ShapeDtypeStruct((count, LANES), jnp.float32),
        ]
        scratch = [pltpu.VMEM((count, panels * order), jnp.float32)]
    else:
        in_specs.append(pl.BlockSpec(memory_space=pl.ANY))
        args.append(partial)
        aliases = {len(args): 0}
    return pl.pallas_call(
        kernel,
        grid_spec=pltpu.PrefetchScalarGridSpec(
            num_scalar_prefetch=1,
            grid=(steps,),
            in_specs=in_specs,
            out_specs=out_specs,
            scratch_shapes=scratch,
        ),
        out_shape=out_shape,
        input_output_aliases=aliases,
        name="finish",
    )(place, *args)


def after(value, *before):
    return lax.optimization_barrier((value, *before))[0]


def per_device(
    old_vectors,
    reflectors,
    triangles,
    pole_sq,
    coupling,
    deflated,
    pole_order,
    anchors,
    root_fraction,
):
    side_index = lax.axis_index("side").astype(jnp.int32)
    row_index = lax.axis_index("row").astype(jnp.int32)
    col_index = lax.axis_index("col").astype(jnp.int32)
    row_count, col_count = lax.axis_size("row"), lax.axis_size("col")
    half_rows, slow = row_count // 2, col_count // 2
    old = old_vectors[0]
    col_width = old.shape[1]
    order_size = pole_sq.shape[0]
    count = anchors.shape[0] // col_count
    panel_local = reflectors[0]
    panels = panel_local.shape[0]
    pairs = [(later, earlier) for later in range(panels) for earlier in range(later)]

    def swap(x, axis, mask):
        size = lax.axis_size(axis)
        return lax.ppermute(x, axis, [(i, i ^ mask) for i in range(size)])

    pieces = [panel_local] + [None] * (col_count - 1)
    pieces[slow] = swap(panel_local, "col", slow)
    for fast in range(1, slow):
        pieces[fast] = swap(panel_local, "col", fast)
        pieces[slow + fast] = swap(pieces[slow], "col", fast)

    first_column = row_index // half_rows * (order_size // 2) + col_index * col_width
    place = jnp.stack([first_column, side_index])
    here = jnp.stack([col_index, row_index])
    col_tables = column_tables(place, pole_order, pole_sq, coupling, deflated, col_width)
    tables = [x.reshape(order_size // LANES, LANES) for x in (pole_sq, deflated, pole_order)]
    anchors3 = anchors.reshape(col_count, 1, count)
    fraction3 = root_fraction.reshape(col_count, 1, count)
    slots = [k + s for s in range(1, slow) for k in (slow, 0)] + [slow, 0]
    mix, squares, dead = mixing_rows(place, col_index, slots, anchors3, fraction3, tables, col_tables)
    half_squares = squares[-1]
    for n, k in enumerate(slots[:-1]):
        half_squares = half_squares + swap(squares[n], "col", k)
    other_squares = swap(half_squares, "row", half_rows)

    size = old.shape[0]
    chunk = size // 4
    far, own, near = [], [], []
    for n in range(4):
        sent, keep_far, keep_own = merge(mix, old, n * chunk, chunk, (count, count))
        got = None
        for fast in range(1, slow):
            part = swap(sent[(fast - 1) * 2 * count : fast * 2 * count], "col", fast)
            got = part if got is None else got + part
        far.append(keep_far)
        own.append(keep_own)
        near.append(got)

    def far_sum(n, lane, length):
        lanes = slice(lane, lane + length)
        return far[n][:, lanes] + near[n][:count, lanes]

    gram = panel_products(here, pieces, row_count, pairs)
    half = chunk // 2
    spans = [(0, 0, chunk), (1, 0, chunk), (2, 0, half), (2, half, half), (3, 0, half), (3, half, half)]
    whole_far = [far_sum(n, 0, chunk) for n in range(4)]
    early = 3
    cut = [whole_far[n] if length == chunk else whole_far[n][:, lane : lane + length] for n, lane, length in spans]
    arrived = []
    for n in range(early):
        arrived.append(swap(cut[n], "col", slow))
    (acc,) = project(
        here, [(whole_far[n], own[n], near[n]) for n in range(3)], 0, pieces, row_count, None, False
    )
    far_proj, own_proj = project(
        here, [(whole_far[3], own[3], near[3])], 3 * chunk, pieces, row_count, acc, True
    )

    gram_sum = gram[0].astype(jnp.float32)
    far_total = far_proj[0].astype(jnp.float32)
    shares = [own_proj[0]]
    for t in range(1, row_count):
        gram_sum = gram_sum + swap(gram[t], "row", t).astype(jnp.float32)
        far_total = far_total + swap(far_proj[t], "row", t).astype(jnp.float32)
    far_total = far_total.astype(jnp.bfloat16)
    for t in range(1, row_count):
        shares.append(swap(own_proj[t], "row", t))
    gram_sum = gram_sum.astype(jnp.bfloat16)
    gram_rows = jnp.stack([gram_sum] + [swap(gram_sum, "row", t) for t in range(1, row_count)])
    grams = [None] * col_count
    grams[0], grams[slow] = gram_rows, swap(gram_rows, "col", slow)
    for fast in range(1, slow):
        grams[fast] = swap(gram_rows, "col", fast)
        grams[slow + fast] = swap(grams[slow], "col", fast)
    shares.append(swap(far_total, "col", slow))
    for n in range(early, len(spans)):
        arrived.append(swap(after(cut[n], far_total), "col", slow))
    coef = coefficients(here, shares, grams, triangles[0], pairs)
    coefs = [coef] + [swap(coef, "row", t) for t in range(1, row_count)]

    def part_of(m):
        n, lane, _ = spans[m]
        return (own[n], near[n], arrived[m], lane)

    starts = [n * chunk + lane for n, lane, _ in spans]
    result, coef_all, scale_all = finish(
        here, [part_of(m) for m in range(4)], 0, pieces, coefs, [half_squares, other_squares, dead[-1]]
    )
    for m in (4, 5):
        (result,) = finish(here, [part_of(m)], starts[m], pieces, [coef_all], [scale_all], result)
    return result[None]


def solution(mesh):
    in_specs = (
        P("side", "row", "col"),
        P("side", None, "row", "col"),
        P("side", None, None, None),
        P(),
        P(),
        P(),
        P(),
        P(),
        P(),
    )
    out_specs = P("side", "col", "row")
    return jax.shard_map(per_device, mesh=mesh, in_specs=in_specs, out_specs=out_specs, check_vma=False)
```

time: 563 us -> 368 us (0.65)
  local copies, waits for them, and re-layouts: 217 us -> 7.87 us
  Pallas kernels: 0 us -> 177 us
  matrix products: 123 us -> 0 us
  starting transfers between devices: 0.3 us -> 43.1 us
  blocking collectives: 35.1 us -> 0 us
  waiting for transfers between devices: 158 us -> 127 us
  between operations: 13.4 us -> 0.25 us
    pallas_call x0 -> x13, Pallas kernels: none -> 177 us  [the longest x4 95 us: merge(): pl.pallas_call(kernel, grid=(size // rows,), in_specs=[pl.BlockSpec((tota...]
    ppermute x0 -> x36, waiting for transfers between devices: none -> 127 us  [swap(): return lax.ppermute(x, axis, [(i, i ^ mask) for i in range(size)])]
    dot_general x9 -> x0, matrix products: 123 us -> none  [the longest x1 78.1 us: per_device(): jnp.einsum('ck,rc->kr', mixing, old_block, preferred_element_type=jnp.flo...]
    scatter x1 -> x0, local copies, waits for them, and re-layouts: 120 us -> none  [per_device(): position = jnp.zeros((order_size,), jnp.int32).at[pole_order].set(jnp.ara...]
    reduce_scatter x1 -> x0, waiting for transfers between devices: 108 us -> none  [per_device(): lax.psum_scatter(jnp.einsum('ck,rc->kr', mixing, old_block, preferred_ele...]
    gather x7 -> x0, local copies, waits for them, and re-layouts: 93.7 us -> none  [the longest x1 23 us: per_device(): col_live = (1 - deflated[sorted_pos]).astype(jnp.float32)]
    psum x1 -> x0, waiting for transfers between devices: 49.9 us -> none  [per_device(): lax.psum(raw_proj.astype(jnp.bfloat16), 'row').astype(jnp.float32)]
    ppermute x0 -> x36, starting transfers between devices: none -> 43.1 us  [swap(): return lax.ppermute(x, axis, [(i, i ^ mask) for i in range(size)])]
  transfers between devices with their start and end apart: 3 -> 36, of which waited for: 2 -> 13; matrix products, arithmetic and copies ran while one was open for 57% -> 5% of each run, Pallas kernels for 0% -> 47%
where the time goes in v1:
time: 368 us; the launch traced here: 367 us
  Pallas kernels  177 us (48%)
  waiting for transfers between devices  127 us (35%)
  starting transfers between devices  43.1 us (12%)
  other arithmetic  11.6 us (3%)
  local copies, waits for them, and re-layouts  7.87 us (2%)
    ppermute x36, waiting for transfers between devices, swap(): return lax.ppermute(x, axis, [(i, i ^ mask) for i in range(size)])  127 us
    pallas_call x4, Pallas kernels, merge(): pl.pallas_call(kernel, grid=(size // rows,), in_specs=[pl.BlockSpec((tota...  95 us
    ppermute x36, starting transfers between devices, swap(): return lax.ppermute(x, axis, [(i, i ^ mask) for i in range(size)])  43.1 us
    pallas_call x2, Pallas kernels, project(): pl.pallas_call(kernel, grid_spec=pltpu.PrefetchScalarGridSpec(num_scalar_...  23.7 us
    pallas_call x3, Pallas kernels, finish(): pl.pallas_call(kernel, grid_spec=pltpu.PrefetchScalarGridSpec(num_scalar_...  21.5 us
    pallas_call x1, Pallas kernels, mixing_rows(): pl.pallas_call(mixing_kernel, grid_spec=pltpu.PrefetchScalarGridSpec(num_...  15.1 us
    pallas_call x1, Pallas kernels, panel_products(): pl.pallas_call(kernel, grid_spec=pltpu.PrefetchScalarGridSpec(num_scalar_...  8.86 us
    pallas_call x1, Pallas kernels, column_tables(): pl.pallas_call(column_kernel, grid_spec=pltpu.PrefetchScalarGridSpec(num_...  7.5 us
  transfers between devices with their start and end apart: 36, of which 13 were waited for; matrix products, arithmetic and copies ran while one was open for 5% of the time, Pallas kernels for 47%

profile of v1, /device:TPU:0, one launch (start us, length us, event | category | flops | bytes accessed | tf_op | source)
XLA Modules:
  0.0 367.0 jit_solution(134058063712417436)
XLA Ops:
  0.0 3.0 collective-permute-start.2
  3.0 0.6 pad_add_fusion.2.place_ref
  3.6 0.7 broadcast_xor_fusion
  4.3 89.6 %collective-permute-done.2.refs_11_.refs_5_.refs_2_.refs_14_ = bf16[2,8192,128]{2,1,0:T(8,128)(2,1)} collective-permute-done((bf16[2,8192,128]{2,1,0:T(8,128)(2,1)}, bf16[2,8192,128]{2,1,0:T(8,128)(2,1)}, u32[]{:S(2)}, u32[]{:S(2)}) %collective-permute-start.2) | collective-permute-done | bytes 4194336 | tf_op jit(solution)/shard_map/ppermute | solution.py:524
  93.9 0.7 pad_add_fusion.1.place_ref
  94.5 7.5 %columns.1 = (f32[32,128]{1,0:T(8,128)}, f32[32,128]{1,0:T(8,128)}) custom-call(s32[2]{0:T(128)} %pad_add_fusion.2.place_ref, s32[1,32768]{1,0:T(1,128)} %bitcast.76, f32[1,32768]{1,0:T(1,128)} %bitcast.72, f32[1,32768]{1,0:T(1,128)} %bitcast.78, s32[1,32768]{1,0:T(1,128)} %bitcast.74), custom_call_target="tpu_custom_call" | custom-call | tf_op jit(solution)/shard_map/columns/pallas_call | solution.py:80
  102.0 15.1 %mixing.1 = (bf16[1024,4096]{1,0:T(8,128)(2,1)}, f32[4,1,256]{2,1,0:T(1,128)}, f32[4,1,256]{2,1,0:T(1,128)}) custom-call(s32[6]{0:T(128)} %pad_add_fusion.1.place_ref, s32[4,1,256]{2,1,0:T(1,128)} %bitcast.83, f32[4,1,256]{2,1,0:T(1,128)} %bitcast.84, f32[256,128]{1,0:T(8,128)} %bitcast.73, s32[256,128]{1,0:T(8,128)} %bitcast.75, s32[256,128]{1,0:T(8,128)} %bitcast.77, ...), custom_call_target="tpu_custom_call" | custom-call | tf_op jit(solution)/shard_map/mixing/pallas_call | solution.py:166
  117.1 23.8 %merge.7 = (bf16[512,2048]{1,0:T(8,128)(2,1)}, bf16[256,2048]{1,0:T(8,128)(2,1)}, bf16[256,2048]{1,0:T(8,128)(2,1)}) custom-call(bf16[1024,4096]{1,0:T(8,128)(2,1)} %get-tuple-element.32.mix_ref, bf16[8192,4096]{1,0:T(8,128)(2,1)} %bitcast.13.old_ref), custom_call_target="tpu_custom_call" | custom-call | tf_op jit(solution)/shard_map/merge/pallas_call | solution.py:195
  140.9 0.5 collective-permute-start.6
  141.4 23.7 %merge.4 = (bf16[512,2048]{1,0:T(8,128)(2,1)}, bf16[256,2048]{1,0:T(8,128)(2,1)}, bf16[256,2048]{1,0:T(8,128)(2,1)}) custom-call(bf16[1024,4096]{1,0:T(8,128)(2,1)} %get-tuple-element.32.mix_ref, bf16[8192,4096]{1,0:T(8,128)(2,1)} %bitcast.13.old_ref), custom_call_target="tpu_custom_call" | custom-call | tf_op jit(solution)/shard_map/merge/pallas_call | solution.py:195
  165.1 1.8 collective-permute-start.33
  166.9 1.8 collective-permute-done.33
  168.7 1.2 collective-permute-done.32
  169.9 1.5 collective-permute-start.31
  171.4 23.8 %merge.5 = (bf16[512,2048]{1,0:T(8,128)(2,1)}, bf16[256,2048]{1,0:T(8,128)(2,1)}, bf16[256,2048]{1,0:T(8,128)(2,1)}) custom-call(bf16[1024,4096]{1,0:T(8,128)(2,1)} %get-tuple-element.32.mix_ref, bf16[8192,4096]{1,0:T(8,128)(2,1)} %bitcast.13.old_ref), custom_call_target="tpu_custom_call" | custom-call | tf_op jit(solution)/shard_map/merge/pallas_call | solution.py:195
  195.6 23.7 %merge.6 = (bf16[512,2048]{1,0:T(8,128)(2,1)}, bf16[256,2048]{1,0:T(8,128)(2,1)}, bf16[256,2048]{1,0:T(8,128)(2,1)}) custom-call(bf16[1024,4096]{1,0:T(8,128)(2,1)} %get-tuple-element.32.mix_ref, bf16[8192,4096]{1,0:T(8,128)(2,1)} %bitcast.13.old_ref), custom_call_target="tpu_custom_call" | custom-call | tf_op jit(solution)/shard_map/merge/pallas_call | solution.py:195
  219.4 0.7 pad_add_fusion.sc_ref
  220.3 1.4 slice_add_fusion.refs_6_
  221.7 1.1 fusion.9
  222.9 2.7 collective-permute-start.34
  225.5 1.1 slice_add_fusion.3.refs_0_
  227.1 2.3 slice_add_fusion.2.refs_0_
  229.5 8.9 %gram.1 = bf16[4,1,128,128]{3,2,1,0:T(8,128)(2,1)} custom-call(s32[2]{0:T(128)} %pad_add_fusion.sc_ref, bf16[2,8192,128]{2,1,0:T(8,128)(2,1)} %bitcast.65, bf16[2,8192,128]{2,1,0:T(8,128)(2,1)} %collective-permute-done.1.refs_10_.refs_4_.refs_1_.refs_13_, bf16[2,8192,128]{2,1,0:T(8,128)(2,1)} %collective-permute-done.2.refs_11_.refs_5_.refs_2_.refs_14_, ...), custom_call_target="tpu_custom_call" | custom-call | tf_op jit(solution)/shard_map/gram/pallas_call | solution.py:326
  238.4 0.8 slice_bitcast_fusion.9
  239.2 1.4 collective-permute-start.21
  240.6 1.7 collective-permute-start.20
  242.2 1.3 collective-permute-start.19
  243.6 2.4 slice_add_fusion.1.refs_3_
  246.0 15.7 %project.2.refs_7_ = f32[2,512,512]{2,1,0:T(8,128)} custom-call(s32[2]{0:T(128)} %pad_add_fusion.sc_ref, bf16[256,2048]{1,0:T(8,128)(2,1)} %slice_add_fusion.2.refs_0_, bf16[256,2048]{1,0:T(8,128)(2,1)} %get-tuple-element.38.refs_1_.refs_0_, bf16[512,2048]{1,0:T(8,128)(2,1)} %collective-permute-done.4.refs_2_.refs_1_, ...), custom_call_target="tpu_custom_call" | custom-call | tf_op jit(solution)/shard_map/project/pallas_call | solution.py:284
  261.7 8.0 %project.3 = (bf16[4,64,1024]{2,1,0:T(8,128)(2,1)}, bf16[4,64,1024]{2,1,0:T(8,128)(2,1)}) custom-call(s32[2]{0:T(128)} %pad_add_fusion.sc_ref, bf16[256,2048]{1,0:T(8,128)(2,1)} %slice_add_fusion.3.refs_0_, bf16[256,2048]{1,0:T(8,128)(2,1)} %get-tuple-element.33.refs_1_.refs_0_, bf16[512,2048]{1,0:T(8,128)(2,1)} %copy-done, bf16[2,8192,128]{2,1,0:T(8,128)(2,1)} %bitcast.67, ...), custom_call_target="tpu_custom_call" | custom-call | tf_op jit(solution)/shard_map/project/pallas_call | solution.py:284
  269.7 1.6 collective-permute-start.11
  271.8 0.8 fusion.5
  272.6 1.4 collective-permute-start.24
  274.0 1.1 slice_bitcast_fusion.6
  275.1 2.5 collective-permute-start.9
  277.7 1.2 collective-permute-done.24
  278.9 0.7 collective-permute-start.22
  279.6 1.8 slice_bitcast_fusion
  281.4 2.2 collective-permute-done.23
  284.0 2.3 collective-permute-start.7
  286.4 4.1 %collective-permute-done.8 = bf16[64,1024]{1,0:T(8,128)(2,1)S(1)} collective-permute-done((bf16[64,1024]{1,0:T(8,128)(2,1)S(1)}, bf16[64,1024]{1,0:T(8,128)(2,1)S(1)}, u32[]{:S(2)}, u32[]{:S(2)}) %collective-permute-start.8) | collective-permute-done | bytes 131104 | tf_op jit(solution)/shard_map/ppermute | solution.py:524
  290.4 0.8 collective-permute-start.16
  291.3 2.2 collective-permute-done.7
  293.4 1.2 collective-permute-start.17
  295.0 4.4 %collective-permute-start.26 = (bf16[4,1,128,128]{3,2,1,0:T(8,128)(2,1)S(1)}, bf16[4,1,128,128]{3,2,1,0:T(8,128)(2,1)S(1)}, u32[]{:S(2)}, u32[]{:S(2)}) collective-permute-start(bf16[4,1,128,128]{3,2,1,0:T(8,128)(2,1)S(1)} %pad_maximum_fusion.refs_5_), channel_id=1, source_target_pairs={{0,2},{1,3},{2,0},{3,1},{4,6},{5,7},{6,4},{7,5},{8,10},{9,11},{10,... | collective-permute-start | bytes 393224 | tf_op jit(solution)/shard_map/ppermute | solution.py:524
  299.4 1.0 fusion.2
  300.3 0.6 collective-permute-done.16.refs_2_
  300.9 4.2 %collective-permute-start.18 = (bf16[64,1024]{1,0:T(8,128)(2,1)S(1)}, bf16[64,1024]{1,0:T(8,128)(2,1)S(1)}, u32[]{:S(2)}, u32[]{:S(2)}) collective-permute-start(bf16[64,1024]{1,0:T(8,128)(2,1)S(1)} %fusion.2), channel_id=1, source_target_pairs={{0,2},{1,3},{2,0},{3,1},{4,6},{5,7},{6,4},{7,5},{8,10},{9,11},{10,... | collective-permute-start | bytes 393224 | tf_op jit(solution)/shard_map/ppermute | solution.py:524
  305.2 15.2 %collective-permute-done.26.refs_7_ = bf16[4,1,128,128]{3,2,1,0:T(8,128)(2,1)S(1)} collective-permute-done((bf16[4,1,128,128]{3,2,1,0:T(8,128)(2,1)S(1)}, bf16[4,1,128,128]{3,2,1,0:T(8,128)(2,1)S(1)}, u32[]{:S(2)}, u32[]{:S(2)}) %collective-permute-start.26) | collective-permute-done | bytes 131104 | tf_op jit(solution)/shard_map/ppermute | solution.py:524
  320.4 1.1 fusion.8
  321.6 1.6 collective-permute-start.14
  323.7 1.6 collective-permute-start.10
  325.3 5.6 %coefficients.1.refs_16_ = bf16[64,1024]{1,0:T(8,128)(2,1)} custom-call(s32[2]{0:T(128)} %pad_add_fusion.sc_ref, bf16[64,1024]{1,0:T(8,128)(2,1)} %get-tuple-element.62.refs_0_, bf16[64,1024]{1,0:T(8,128)(2,1)} %copy-done.14, bf16[64,1024]{1,0:T(8,128)(2,1)} %copy-done.15, bf16[64,1024]{1,0:T(8,128)(2,1)} %copy-done.16, bf16[64,1024]{1,0:T(8,128)(2,1)} %copy-done.19, ...), custom_call_target="tpu_custom_call" | custom-call | tf_op jit(solution)/shard_map/coefficients/pallas_call | solution.py:380
  330.9 0.7 collective-permute-start.28
  331.7 1.2 collective-permute-start.29
  332.9 4.9 %collective-permute-done.28.refs_17_ = bf16[64,1024]{1,0:T(8,128)(2,1)S(1)} collective-permute-done((bf16[64,1024]{1,0:T(8,128)(2,1)}, bf16[64,1024]{1,0:T(8,128)(2,1)S(1)}, u32[]{:S(2)}, u32[]{:S(2)}) %collective-permute-start.28) | collective-permute-done | bytes 131104 | tf_op jit(solution)/shard_map/ppermute | solution.py:524
  337.8 2.3 collective-permute-start.30
  340.1 1.3 slice_bitcast_fusion.11.refs_22_
  341.3 1.6 collective-permute-done.29.refs_18_
  342.9 1.9 collective-permute-done.30.refs_19_
  344.9 0.6 copy-done.13
  345.5 12.8 %finish.3 = (bf16[256,8192]{1,0:T(8,128)(2,1)}, bf16[256,1024]{1,0:T(8,128)(2,1)}, f32[256,128]{1,0:T(8,128)}) custom-call(s32[2]{0:T(128)} %pad_add_fusion.sc_ref, bf16[256,2048]{1,0:T(8,128)(2,1)} %get-tuple-element.38.refs_1_.refs_0_, bf16[512,2048]{1,0:T(8,128)(2,1)} %collective-permute-done.4.refs_2_.refs_1_, bf16[256,2048]{1,0:T(8,128)(2,1)} %copy-done.5, ...), custom_call_target="tpu_custom_call" | custom-call | tf_op jit(solution)/shard_map/finish/pallas_call | solution.py:479
  358.3 4.4 %finish.4.refs_9_ = bf16[256,8192]{1,0:T(8,128)(2,1)} custom-call(s32[2]{0:T(128)} %pad_add_fusion.sc_ref, bf16[256,2048]{1,0:T(8,128)(2,1)} %get-tuple-element.33.refs_1_.refs_0_, bf16[512,2048]{1,0:T(8,128)(2,1)} %copy-done, bf16[256,1024]{1,0:T(8,128)(2,1)} %collective-permute-done.35.refs_2_, ...), custom_call_target="tpu_custom_call", output_to_operand_aliasing={{}: (10, {})} | custom-call | tf_op jit(solution)/shard_map/finish/pallas_call | solution.py:479
  362.7 4.4 %finish.5 = bf16[256,8192]{1,0:T(8,128)(2,1)} custom-call(s32[2]{0:T(128)} %pad_add_fusion.sc_ref, bf16[256,2048]{1,0:T(8,128)(2,1)} %get-tuple-element.33.refs_1_.refs_0_, bf16[512,2048]{1,0:T(8,128)(2,1)} %copy-done, bf16[256,1024]{1,0:T(8,128)(2,1)} %collective-permute-done.10.refs_2_, ...), custom_call_target="tpu_custom_call", output_to_operand_aliasing={{}: (10, {})} | custom-call | tf_op jit(solution)/shard_map/finish/pallas_call | solution.py:479
  (88 shorter events, 3.3 us)
Async XLA Ops:
  0.0 93.9 %collective-permute-start.2 = (bf16[2,8192,128]{2,1,0:T(8,128)(2,1)}, bf16[2,8192,128]{2,1,0:T(8,128)(2,1)}, u32[]{:S(2)}, u32[]{:S(2)}) collective-permute-start(bf16[2,8192,128]{2,1,0:T(8,128)(2,1)} %bitcast.63), channel_id=1, source_target_pairs={{0,2},{1,3},{2,0},{3,1},{4,6},{5,7},{6,4},{7,5},{8,10},{9,11},{10,... | collective-permute-start | bytes 12582920 | tf_op jit(solution)/shard_map/ppermute | solution.py:524
  3.0 226.5 %collective-permute-start.1 = (bf16[2,8192,128]{2,1,0:T(8,128)(2,1)}, bf16[2,8192,128]{2,1,0:T(8,128)(2,1)}, u32[]{:S(2)}, u32[]{:S(2)}) collective-permute-start(bf16[2,8192,128]{2,1,0:T(8,128)(2,1)} %bitcast.64), channel_id=1, source_target_pairs={{0,1},{1,0},{2,3},{3,2},{4,5},{5,4},{6,7},{7,6},{8,9},{9,8},{10,11... | collective-permute-start | bytes 12582920 | tf_op jit(solution)/shard_map/ppermute | solution.py:524
  93.9 135.6 %collective-permute-start.3 = (bf16[2,8192,128]{2,1,0:T(8,128)(2,1)}, bf16[2,8192,128]{2,1,0:T(8,128)(2,1)}, u32[]{:S(2)}, u32[]{:S(2)}) collective-permute-start(bf16[2,8192,128]{2,1,0:T(8,128)(2,1)} %collective-permute-done.2.refs_11_.refs_5_.refs_2_.refs_14_), channel_id=1, source_target_pairs={{0,1},{1,0},{2,3},{3,2},{4,5},{5,4},{6,7},{7,6},{8,9},{9,8},{10,11... | collective-permute-start | bytes 12582920 | tf_op jit(solution)/shard_map/ppermute | solution.py:524
  140.9 24.2 %copy-start.22 = (f32[4,1,256]{2,1,0:T(1,128)S(1)}, f32[4,1,256]{2,1,0:T(1,128)}, u32[]{:S(2)}) copy-start(f32[4,1,256]{2,1,0:T(1,128)} %get-tuple-element.49) | copy-start | bytes 12292
  140.9 79.1 %collective-permute-start.6 = (bf16[512,2048]{1,0:T(8,128)(2,1)}, bf16[512,2048]{1,0:T(8,128)(2,1)}, u32[]{:S(2)}, u32[]{:S(2)}) collective-permute-start(bf16[512,2048]{1,0:T(8,128)(2,1)} %get-tuple-element.43), channel_id=1, source_target_pairs={{0,1},{1,0},{2,3},{3,2},{4,5},{5,4},{6,7},{7,6},{8,9},{9,8},{10,11... | collective-permute-start | bytes 6291464 | tf_op jit(solution)/shard_map/ppermute | solution.py:524
  165.1 57.8 %collective-permute-start = (bf16[512,2048]{1,0:T(8,128)(2,1)}, bf16[512,2048]{1,0:T(8,128)(2,1)S(1)}, u32[]{:S(2)}, u32[]{:S(2)}) collective-permute-start(bf16[512,2048]{1,0:T(8,128)(2,1)} %get-tuple-element.34), channel_id=1, source_target_pairs={{0,1},{1,0},{2,3},{3,2},{4,5},{5,4},{6,7},{7,6},{8,9},{9,8},{10,11... | collective-permute-start | bytes 6291464 | tf_op jit(solution)/shard_map/ppermute | solution.py:524
  165.1 3.6 collective-permute-start.33
  168.7 1.2 collective-permute-start.32
  169.9 25.3 %collective-permute-start.31 = (f32[1,256]{1,0:T(1,128)S(1)}, f32[1,256]{1,0:T(1,128)S(1)}, u32[]{:S(2)}, u32[]{:S(2)}) collective-permute-start(f32[1,256]{1,0:T(1,128)S(1)} %get-tuple-element.69), channel_id=1, source_target_pairs={{0,3},{1,2},{2,1},{3,0},{4,7},{5,6},{6,5},{7,4},{8,11},{9,10},{10,... | collective-permute-start | bytes 3080 | tf_op jit(solution)/shard_map/ppermute | solution.py:524
  195.2 25.1 %copy-start.7 = (bf16[256,2048]{1,0:T(8,128)(2,1)S(1)}, bf16[256,2048]{1,0:T(8,128)(2,1)}, u32[]{:S(2)}) copy-start(bf16[256,2048]{1,0:T(8,128)(2,1)} %get-tuple-element.42) | copy-start | bytes 3145732
  195.2 31.4 %collective-permute-start.4 = (bf16[512,2048]{1,0:T(8,128)(2,1)}, bf16[512,2048]{1,0:T(8,128)(2,1)}, u32[]{:S(2)}, u32[]{:S(2)}) collective-permute-start(bf16[512,2048]{1,0:T(8,128)(2,1)} %get-tuple-element.37), channel_id=1, source_target_pairs={{0,1},{1,0},{2,3},{3,2},{4,5},{5,4},{6,7},{7,6},{8,9},{9,8},{10,11... | collective-permute-start | bytes 6291464 | tf_op jit(solution)/shard_map/ppermute | solution.py:524
  220.0 22.2 %collective-permute-start.5 = (bf16[512,2048]{1,0:T(8,128)(2,1)}, bf16[512,2048]{1,0:T(8,128)(2,1)}, u32[]{:S(2)}, u32[]{:S(2)}) collective-permute-start(bf16[512,2048]{1,0:T(8,128)(2,1)} %get-tuple-element.40), channel_id=1, source_target_pairs={{0,1},{1,0},{2,3},{3,2},{4,5},{5,4},{6,7},{7,6},{8,9},{9,8},{10,11... | collective-permute-start | bytes 6291464 | tf_op jit(solution)/shard_map/ppermute | solution.py:524
  220.3 2.6 copy-start.21
  220.3 5.3 %copy-start.6 = (bf16[256,2048]{1,0:T(8,128)(2,1)S(1)}, bf16[256,2048]{1,0:T(8,128)(2,1)}, u32[]{:S(2)}) copy-start(bf16[256,2048]{1,0:T(8,128)(2,1)} %get-tuple-element.35) | copy-start | bytes 3145732
  221.7 4.9 %copy-start.2 = (bf16[256,2048]{1,0:T(8,128)(2,1)}, bf16[256,2048]{1,0:T(8,128)(2,1)S(1)}, u32[]{:S(2)}) copy-start(bf16[256,2048]{1,0:T(8,128)(2,1)S(1)} %slice_add_fusion.refs_6_) | copy-start | bytes 3145732
  222.9 4.3 %copy-start.9 = (bf16[256,2048]{1,0:T(8,128)(2,1)S(1)}, bf16[256,2048]{1,0:T(8,128)(2,1)}, u32[]{:S(2)}) copy-start(bf16[256,2048]{1,0:T(8,128)(2,1)} %get-tuple-element.36) | copy-start | bytes 3145732
  222.9 6.6 %copy-start = (bf16[512,2048]{1,0:T(8,128)(2,1)}, bf16[512,2048]{1,0:T(8,128)(2,1)S(1)}, u32[]{:S(2)}) copy-start(bf16[512,2048]{1,0:T(8,128)(2,1)S(1)} %collective-permute-done.refs_2_.refs_1_) | copy-start | bytes 6291460
  222.9 52.2 %collective-permute-start.34 = (f32[1,256]{1,0:T(1,128)S(1)}, f32[1,256]{1,0:T(1,128)S(1)}, u32[]{:S(2)}, u32[]{:S(2)}) collective-permute-start(f32[1,256]{1,0:T(1,128)S(1)} %fusion.7.refs_20_), channel_id=1, source_target_pairs={{0,8},{4,12},{8,0},{12,4},{1,9},{5,13},{9,1},{13,5},{2,10},{6,14},... | collective-permute-start | bytes 3080 | tf_op jit(solution)/shard_map/ppermute | solution.py:524
  226.6 51.0 %collective-permute-start.13 = (bf16[256,1024]{1,0:T(8,128)(2,1)}, bf16[256,1024]{1,0:T(8,128)(2,1)}, u32[]{:S(2)}, u32[]{:S(2)}) collective-permute-start(bf16[256,1024]{1,0:T(8,128)(2,1)} %get-tuple-element.58), channel_id=1, source_target_pairs={{0,2},{1,3},{2,0},{3,1},{4,6},{5,7},{6,4},{7,5},{8,10},{9,11},{10,... | collective-permute-start | bytes 1572872 | tf_op jit(solution)/shard_map/ppermute | solution.py:524
  229.5 14.1 %copy-start.8 = (bf16[256,2048]{1,0:T(8,128)(2,1)S(1)}, bf16[256,2048]{1,0:T(8,128)(2,1)}, u32[]{:S(2)}) copy-start(bf16[256,2048]{1,0:T(8,128)(2,1)} %get-tuple-element.39) | copy-start | bytes 3145732
  239.2 30.6 %collective-permute-start.21 = (bf16[1,128,128]{2,1,0:T(8,128)(2,1)S(1)}, bf16[1,128,128]{2,1,0:T(8,128)(2,1)S(1)}, u32[]{:S(2)}, u32[]{:S(2)}) collective-permute-start(bf16[1,128,128]{2,1,0:T(8,128)(2,1)S(1)} %get-tuple-element.67), channel_id=1, source_target_pairs={{0,12},{4,8},{8,4},{12,0},{1,13},{5,9},{9,5},{13,1},{2,14},{6,10},... | collective-permute-start | bytes 98312 | tf_op jit(solution)/shard_map/ppermute | solution.py:524
  240.6 30.8 %collective-permute-start.20 = (bf16[1,128,128]{2,1,0:T(8,128)(2,1)S(1)}, bf16[1,128,128]{2,1,0:T(8,128)(2,1)S(1)}, u32[]{:S(2)}, u32[]{:S(2)}) collective-permute-start(bf16[1,128,128]{2,1,0:T(8,128)(2,1)S(1)} %get-tuple-element.68), channel_id=1, source_target_pairs={{0,8},{4,12},{8,0},{12,4},{1,9},{5,13},{9,1},{13,5},{2,10},{6,14},... | collective-permute-start | bytes 98312 | tf_op jit(solution)/shard_map/ppermute | solution.py:524
  242.2 29.6 %collective-permute-start.19 = (bf16[1,128,128]{2,1,0:T(8,128)(2,1)S(1)}, bf16[1,128,128]{2,1,0:T(8,128)(2,1)S(1)}, u32[]{:S(2)}, u32[]{:S(2)}) collective-permute-start(bf16[1,128,128]{2,1,0:T(8,128)(2,1)S(1)} %get-tuple-element.66), channel_id=1, source_target_pairs={{0,4},{4,0},{8,12},{12,8},{1,5},{5,1},{9,13},{13,9},{2,6},{6,2},{1... | collective-permute-start | bytes 98312 | tf_op jit(solution)/shard_map/ppermute | solution.py:524
  261.7 8.1 %copy-start.3 = (bf16[256,2048]{1,0:T(8,128)(2,1)S(1)}, bf16[256,2048]{1,0:T(8,128)(2,1)}, u32[]{:S(2)}) copy-start(bf16[256,2048]{1,0:T(8,128)(2,1)} %slice_add_fusion.2.refs_0_) | copy-start | bytes 3145732
  261.7 9.7 %copy-start.4 = (bf16[256,2048]{1,0:T(8,128)(2,1)S(1)}, bf16[256,2048]{1,0:T(8,128)(2,1)}, u32[]{:S(2)}) copy-start(bf16[256,2048]{1,0:T(8,128)(2,1)} %slice_add_fusion.1.refs_3_) | copy-start | bytes 3145732
  269.7 50.7 %copy-start.1 = (bf16[256,2048]{1,0:T(8,128)(2,1)S(1)}, bf16[256,2048]{1,0:T(8,128)(2,1)}, u32[]{:S(2)}) copy-start(bf16[256,2048]{1,0:T(8,128)(2,1)} %slice_add_fusion.3.refs_0_) | copy-start | bytes 3145732
  269.7 61.2 %collective-permute-start.11 = (bf16[256,2048]{1,0:T(8,128)(2,1)S(1)}, bf16[256,2048]{1,0:T(8,128)(2,1)S(1)}, u32[]{:S(2)}, u32[]{:S(2)}) collective-permute-start(bf16[256,2048]{1,0:T(8,128)(2,1)S(1)} %copy-done.3), channel_id=1, source_target_pairs={{0,2},{1,3},{2,0},{3,1},{4,6},{5,7},{6,4},{7,5},{8,10},{9,11},{10,... | collective-permute-start | bytes 3145736 | tf_op jit(solution)/shard_map/ppermute | solution.py:524
  271.3 60.3 %collective-permute-start.12 = (bf16[256,2048]{1,0:T(8,128)(2,1)S(1)}, bf16[256,2048]{1,0:T(8,128)(2,1)}, u32[]{:S(2)}, u32[]{:S(2)}) collective-permute-start(bf16[256,2048]{1,0:T(8,128)(2,1)S(1)} %copy-done.4), channel_id=1, source_target_pairs={{0,2},{1,3},{2,0},{3,1},{4,6},{5,7},{6,4},{7,5},{8,10},{9,11},{10,... | collective-permute-start | bytes 3145736 | tf_op jit(solution)/shard_map/ppermute | solution.py:524
  272.6 6.3 %collective-permute-start.24 = (bf16[1,128,128]{2,1,0:T(8,128)(2,1)S(1)}, bf16[1,128,128]{2,1,0:T(8,128)(2,1)S(1)}, u32[]{:S(2)}, u32[]{:S(2)}) collective-permute-start(bf16[1,128,128]{2,1,0:T(8,128)(2,1)S(1)} %fusion.5), channel_id=1, source_target_pairs={{0,12},{4,8},{8,4},{12,0},{1,13},{5,9},{9,5},{13,1},{2,14},{6,10},... | collective-permute-start | bytes 98312 | tf_op jit(solution)/shard_map/ppermute | solution.py:524
  275.1 55.8 %copy-start.23 = (f32[1,256]{1,0:T(1,128)}, f32[1,256]{1,0:T(1,128)S(1)}, u32[]{:S(2)}) copy-start(f32[1,256]{1,0:T(1,128)S(1)} %collective-permute-done.34.refs_21_) | copy-start | bytes 3076
  275.1 11.1 %collective-permute-start.9 = (bf16[64,1024]{1,0:T(8,128)(2,1)S(1)}, bf16[64,1024]{1,0:T(8,128)(2,1)S(1)}, u32[]{:S(2)}, u32[]{:S(2)}) collective-permute-start(bf16[64,1024]{1,0:T(8,128)(2,1)S(1)} %get-tuple-element.64), channel_id=1, source_target_pairs={{0,12},{4,8},{8,4},{12,0},{1,13},{5,9},{9,5},{13,1},{2,14},{6,10},... | collective-permute-start | bytes 393224 | tf_op jit(solution)/shard_map/ppermute | solution.py:524
  277.7 5.9 %collective-permute-start.23 = (bf16[1,128,128]{2,1,0:T(8,128)(2,1)S(1)}, bf16[1,128,128]{2,1,0:T(8,128)(2,1)S(1)}, u32[]{:S(2)}, u32[]{:S(2)}) collective-permute-start(bf16[1,128,128]{2,1,0:T(8,128)(2,1)S(1)} %fusion.5), channel_id=1, source_target_pairs={{0,8},{4,12},{8,0},{12,4},{1,9},{5,13},{9,1},{13,5},{2,10},{6,14},... | collective-permute-start | bytes 98312 | tf_op jit(solution)/shard_map/ppermute | solution.py:524
  278.9 5.1 %collective-permute-start.22 = (bf16[1,128,128]{2,1,0:T(8,128)(2,1)S(1)}, bf16[1,128,128]{2,1,0:T(8,128)(2,1)S(1)}, u32[]{:S(2)}, u32[]{:S(2)}) collective-permute-start(bf16[1,128,128]{2,1,0:T(8,128)(2,1)S(1)} %fusion.5), channel_id=1, source_target_pairs={{0,4},{4,0},{8,12},{12,8},{1,5},{5,1},{9,13},{13,9},{2,6},{6,2},{1... | collective-permute-start | bytes 98312 | tf_op jit(solution)/shard_map/ppermute | solution.py:524
  283.6 6.9 %collective-permute-start.8 = (bf16[64,1024]{1,0:T(8,128)(2,1)S(1)}, bf16[64,1024]{1,0:T(8,128)(2,1)S(1)}, u32[]{:S(2)}, u32[]{:S(2)}) collective-permute-start(bf16[64,1024]{1,0:T(8,128)(2,1)S(1)} %get-tuple-element.65), channel_id=1, source_target_pairs={{0,8},{4,12},{8,0},{12,4},{1,9},{5,13},{9,1},{13,5},{2,10},{6,14},... | collective-permute-start | bytes 393224 | tf_op jit(solution)/shard_map/ppermute | solution.py:524
  284.0 9.4 %collective-permute-start.7 = (bf16[64,1024]{1,0:T(8,128)(2,1)S(1)}, bf16[64,1024]{1,0:T(8,128)(2,1)S(1)}, u32[]{:S(2)}, u32[]{:S(2)}) collective-permute-start(bf16[64,1024]{1,0:T(8,128)(2,1)S(1)} %get-tuple-element.63), channel_id=1, source_target_pairs={{0,4},{4,0},{8,12},{12,8},{1,5},{5,1},{9,13},{13,9},{2,6},{6,2},{1... | collective-permute-start | bytes 393224 | tf_op jit(solution)/shard_map/ppermute | solution.py:524
  286.3 8.7 %collective-permute-start.15 = (bf16[64,1024]{1,0:T(8,128)(2,1)S(1)}, bf16[64,1024]{1,0:T(8,128)(2,1)S(1)}, u32[]{:S(2)}, u32[]{:S(2)}) collective-permute-start(bf16[64,1024]{1,0:T(8,128)(2,1)S(1)} %get-tuple-element.61), channel_id=1, source_target_pairs={{0,4},{4,0},{8,12},{12,8},{1,5},{5,1},{9,13},{13,9},{2,6},{6,2},{1... | collective-permute-start | bytes 393224 | tf_op jit(solution)/shard_map/ppermute | solution.py:524
  286.4 38.9 %copy-start.10 = (bf16[4,1,128,128]{3,2,1,0:T(8,128)(2,1)}, bf16[4,1,128,128]{3,2,1,0:T(8,128)(2,1)S(1)}, u32[]{:S(2)}) copy-start(bf16[4,1,128,128]{3,2,1,0:T(8,128)(2,1)S(1)} %pad_maximum_fusion.refs_5_) | copy-start | bytes 393220
  290.4 10.5 %collective-permute-start.16 = (bf16[64,1024]{1,0:T(8,128)(2,1)S(1)}, bf16[64,1024]{1,0:T(8,128)(2,1)S(1)}, u32[]{:S(2)}, u32[]{:S(2)}) collective-permute-start(bf16[64,1024]{1,0:T(8,128)(2,1)S(1)} %get-tuple-element.60), channel_id=1, source_target_pairs={{0,8},{4,12},{8,0},{12,4},{1,9},{5,13},{9,1},{13,5},{2,10},{6,14},... | collective-permute-start | bytes 393224 | tf_op jit(solution)/shard_map/ppermute | solution.py:524
  293.4 7.5 %collective-permute-start.17 = (bf16[64,1024]{1,0:T(8,128)(2,1)S(1)}, bf16[64,1024]{1,0:T(8,128)(2,1)S(1)}, u32[]{:S(2)}, u32[]{:S(2)}) collective-permute-start(bf16[64,1024]{1,0:T(8,128)(2,1)S(1)} %get-tuple-element.59), channel_id=1, source_target_pairs={{0,12},{4,8},{8,4},{12,0},{1,13},{5,9},{9,5},{13,1},{2,14},{6,10},... | collective-permute-start | bytes 393224 | tf_op jit(solution)/shard_map/ppermute | solution.py:524
  295.0 30.3 %copy-start.14 = (bf16[64,1024]{1,0:T(8,128)(2,1)}, bf16[64,1024]{1,0:T(8,128)(2,1)S(1)}, u32[]{:S(2)}) copy-start(bf16[64,1024]{1,0:T(8,128)(2,1)S(1)} %collective-permute-done.15.refs_1_) | copy-start | bytes 393220
  295.0 25.4 %collective-permute-start.26 = (bf16[4,1,128,128]{3,2,1,0:T(8,128)(2,1)S(1)}, bf16[4,1,128,128]{3,2,1,0:T(8,128)(2,1)S(1)}, u32[]{:S(2)}, u32[]{:S(2)}) collective-permute-start(bf16[4,1,128,128]{3,2,1,0:T(8,128)(2,1)S(1)} %pad_maximum_fusion.refs_5_), channel_id=1, source_target_pairs={{0,2},{1,3},{2,0},{3,1},{4,6},{5,7},{6,4},{7,5},{8,10},{9,11},{10,... | collective-permute-start | bytes 393224 | tf_op jit(solution)/shard_map/ppermute | solution.py:524
  300.9 24.3 %copy-start.15 = (bf16[64,1024]{1,0:T(8,128)(2,1)}, bf16[64,1024]{1,0:T(8,128)(2,1)S(1)}, u32[]{:S(2)}) copy-start(bf16[64,1024]{1,0:T(8,128)(2,1)S(1)} %collective-permute-done.16.refs_2_) | copy-start | bytes 393220
  300.9 20.6 %collective-permute-start.25 = (bf16[4,1,128,128]{3,2,1,0:T(8,128)(2,1)S(1)}, bf16[4,1,128,128]{3,2,1,0:T(8,128)(2,1)S(1)}, u32[]{:S(2)}, u32[]{:S(2)}) collective-permute-start(bf16[4,1,128,128]{3,2,1,0:T(8,128)(2,1)S(1)} %pad_maximum_fusion.refs_5_), channel_id=1, source_target_pairs={{0,1},{1,0},{2,3},{3,2},{4,5},{5,4},{6,7},{7,6},{8,9},{9,8},{10,11... | collective-permute-start | bytes 393224 | tf_op jit(solution)/shard_map/ppermute | solution.py:524
  300.9 19.5 %copy-start.16 = (bf16[64,1024]{1,0:T(8,128)(2,1)}, bf16[64,1024]{1,0:T(8,128)(2,1)S(1)}, u32[]{:S(2)}) copy-start(bf16[64,1024]{1,0:T(8,128)(2,1)S(1)} %collective-permute-done.17.refs_3_) | copy-start | bytes 393220
  300.9 22.2 %collective-permute-start.18 = (bf16[64,1024]{1,0:T(8,128)(2,1)S(1)}, bf16[64,1024]{1,0:T(8,128)(2,1)S(1)}, u32[]{:S(2)}, u32[]{:S(2)}) collective-permute-start(bf16[64,1024]{1,0:T(8,128)(2,1)S(1)} %fusion.2), channel_id=1, source_target_pairs={{0,2},{1,3},{2,0},{3,1},{4,6},{5,7},{6,4},{7,5},{8,10},{9,11},{10,... | collective-permute-start | bytes 393224 | tf_op jit(solution)/shard_map/ppermute | solution.py:524
  320.4 1.1 copy-start.17
  320.4 3.2 collective-permute-start.27
  321.6 2.1 copy-start.18
  321.6 23.3 %collective-permute-start.14 = (bf16[256,1024]{1,0:T(8,128)(2,1)}, bf16[256,1024]{1,0:T(8,128)(2,1)}, u32[]{:S(2)}, u32[]{:S(2)}) collective-permute-start(bf16[256,1024]{1,0:T(8,128)(2,1)} %get-tuple-element.47), channel_id=1, source_target_pairs={{0,2},{1,3},{2,0},{3,1},{4,6},{5,7},{6,4},{7,5},{8,10},{9,11},{10,... | collective-permute-start | bytes 1572872 | tf_op jit(solution)/shard_map/ppermute | solution.py:524
  323.2 2.1 copy-start.19
  323.2 35.1 %collective-permute-start.35 = (bf16[256,1024]{1,0:T(8,128)(2,1)}, bf16[256,1024]{1,0:T(8,128)(2,1)}, u32[]{:S(2)}, u32[]{:S(2)}) collective-permute-start(bf16[256,1024]{1,0:T(8,128)(2,1)} %get-tuple-element.53), channel_id=1, source_target_pairs={{0,2},{1,3},{2,0},{3,1},{4,6},{5,7},{6,4},{7,5},{8,10},{9,11},{10,... | collective-permute-start | bytes 1572872 | tf_op jit(solution)/shard_map/ppermute | solution.py:524
  323.7 1.6 copy-start.20
  323.7 39.0 %collective-permute-start.10 = (bf16[256,1024]{1,0:T(8,128)(2,1)}, bf16[256,1024]{1,0:T(8,128)(2,1)}, u32[]{:S(2)}, u32[]{:S(2)}) collective-permute-start(bf16[256,1024]{1,0:T(8,128)(2,1)} %get-tuple-element.46), channel_id=1, source_target_pairs={{0,2},{1,3},{2,0},{3,1},{4,6},{5,7},{6,4},{7,5},{8,10},{9,11},{10,... | collective-permute-start | bytes 1572872 | tf_op jit(solution)/shard_map/ppermute | solution.py:524
  330.9 14.0 %copy-start.5 = (bf16[256,2048]{1,0:T(8,128)(2,1)}, bf16[256,2048]{1,0:T(8,128)(2,1)S(1)}, u32[]{:S(2)}) copy-start(bf16[256,2048]{1,0:T(8,128)(2,1)S(1)} %collective-permute-done.11.refs_2_) | copy-start | bytes 3145732
  330.9 6.9 %collective-permute-start.28 = (bf16[64,1024]{1,0:T(8,128)(2,1)}, bf16[64,1024]{1,0:T(8,128)(2,1)S(1)}, u32[]{:S(2)}, u32[]{:S(2)}) collective-permute-start(bf16[64,1024]{1,0:T(8,128)(2,1)} %coefficients.1.refs_16_), channel_id=1, source_target_pairs={{0,4},{4,0},{8,12},{12,8},{1,5},{5,1},{9,13},{13,9},{2,6},{6,2},{1... | collective-permute-start | bytes 393224 | tf_op jit(solution)/shard_map/ppermute | solution.py:524
  331.7 11.3 %collective-permute-start.29 = (bf16[64,1024]{1,0:T(8,128)(2,1)}, bf16[64,1024]{1,0:T(8,128)(2,1)S(1)}, u32[]{:S(2)}, u32[]{:S(2)}) collective-permute-start(bf16[64,1024]{1,0:T(8,128)(2,1)} %coefficients.1.refs_16_), channel_id=1, source_target_pairs={{0,8},{4,12},{8,0},{12,4},{1,9},{5,13},{9,1},{13,5},{2,10},{6,14},... | collective-permute-start | bytes 393224 | tf_op jit(solution)/shard_map/ppermute | solution.py:524
  337.8 7.1 %copy-start.11 = (bf16[64,1024]{1,0:T(8,128)(2,1)}, bf16[64,1024]{1,0:T(8,128)(2,1)S(1)}, u32[]{:S(2)}) copy-start(bf16[64,1024]{1,0:T(8,128)(2,1)S(1)} %collective-permute-done.28.refs_17_) | copy-start | bytes 393220
  337.8 7.1 %collective-permute-start.30 = (bf16[64,1024]{1,0:T(8,128)(2,1)}, bf16[64,1024]{1,0:T(8,128)(2,1)S(1)}, u32[]{:S(2)}, u32[]{:S(2)}) collective-permute-start(bf16[64,1024]{1,0:T(8,128)(2,1)} %coefficients.1.refs_16_), channel_id=1, source_target_pairs={{0,12},{4,8},{8,4},{12,0},{1,13},{5,9},{9,5},{13,1},{2,14},{6,10},... | collective-permute-start | bytes 393224 | tf_op jit(solution)/shard_map/ppermute | solution.py:524
  342.9 1.9 copy-start.12
  344.8 0.6 copy-start.13

commit v2 on v1

--- a/solution.py
+++ b/solution.py
@@ -1,3 +1,5 @@
+import math
+
 import jax
 import jax.numpy as jnp
 from jax import lax
@@ -42,13 +44,14 @@
     rows = out_sq_ref.shape[0]
     chunk = order_ref.shape[1]
     local = order_ref[...] - place_ref[0]
-    high = jnp.broadcast_to(local >> 7, (rows, chunk))
-    low = jnp.broadcast_to(local & 127, (LANES, chunk))
-    in_row = high == lax.broadcasted_iota(jnp.int32, (rows, chunk), 0)
-    in_lane = jnp.where(low == lax.broadcasted_iota(jnp.int32, (LANES, chunk), 0), 1.0, 0.0)
+    short = lambda x, height: jnp.broadcast_to(x.astype(jnp.float32).astype(jnp.bfloat16), (height, chunk))
+    count_up = lambda height: short(lax.broadcasted_iota(jnp.int32, (height, chunk), 0), height)
+    zero = jnp.zeros((), jnp.bfloat16)
+    in_row = short(local >> 7, rows) == count_up(rows)
+    in_lane = jnp.where(short(local & 127, LANES) == count_up(LANES), jnp.ones((), jnp.bfloat16), zero)
     num = (1 - deflated_ref[...]).astype(jnp.float32) * coupling_ref[...]
     parts = [
-        jnp.where(in_row, jnp.broadcast_to(part, (rows, chunk)), 0.0).astype(jnp.bfloat16)
+        jnp.where(in_row, short(part, rows), zero)
         for part in split3(sq_ref[...]) + split3(num)
     ]
     add_up(
@@ -56,7 +59,7 @@
         acc_ref,
         lax.dot_general(
             jnp.concatenate(parts, axis=0),
-            in_lane.astype(jnp.bfloat16),
+            in_lane,
             NT,
             preferred_element_type=jnp.float32,
         ),
@@ -74,7 +77,7 @@
 def column_tables(place, pole_order, pole_sq, coupling, deflated, col_width):
     order_size = pole_order.shape[0]
     rows = col_width // LANES
-    chunk = tile_of(order_size, 4096)
+    chunk = tile_of(order_size, 16384)
     row_spec = pl.BlockSpec((1, chunk), lambda i, place: (0, i))
     out_spec = pl.BlockSpec((rows, LANES), lambda i, place: (0, 0))
     return pl.pallas_call(
@@ -151,14 +154,13 @@
     squares_ref[0] = jnp.sum(total.T, axis=0, keepdims=True)
 
 
-def mixing_rows(place, col_index, slots, anchors3, fraction3, tables, col_tables):
+def mixing_rows(place, slots, anchors3, fraction3, tables, col_tables):
     count = anchors3.shape[2]
     rows = col_tables[0].shape[0]
     width = rows * LANES
-    scalars = jnp.concatenate([place, jnp.asarray(slots, jnp.int32) ^ col_index])
 
     def pick(i, sc):
-        return (sc[2 + i], 0, 0)
+        return (sc[4 + i], 0, 0)
 
     row_spec = pl.BlockSpec((1, 1, count), pick)
     whole = lambda a: pl.BlockSpec(a.shape, lambda i, sc: (0,) * a.ndim)
@@ -177,12 +179,12 @@
             jax.ShapeDtypeStruct((len(slots), 1, count), jnp.float32),
         ],
         name="mixing",
-    )(scalars, anchors3, fraction3, *tables, *col_tables)
+    )(place, anchors3, fraction3, *tables, *col_tables)
 
 
 def merge(mix, old, start, size, kept):
     total, depth = mix.shape
-    rows = tile_of(size, 512)
+    rows = tile_of(math.gcd(size, start) if start else size, 512)
     sent = total - kept[0] - kept[1]
     splits = [(0, sent), (sent, kept[0]), (sent + kept[0], kept[1])]
     first = start // rows
@@ -201,6 +203,7 @@
         ],
         out_specs=[pl.BlockSpec((length, rows), lambda i: (0, i)) for _, length in splits],
         out_shape=[jax.ShapeDtypeStruct((length, size), jnp.bfloat16) for _, length in splits],
+        compiler_params=pltpu.CompilerParams(vmem_limit_bytes=40 * 2**20),
         name="merge",
     )(mix, old)
 
@@ -221,7 +224,7 @@
     slots, (panels, _, wide) = len(pieces), pieces[0].shape
     count = parts[0][0].shape[0]
     order = slots * wide
-    tile = tile_of(parts[0][0].shape[1], 1024)
+    tile = tile_of(parts[0][0].shape[1], 2048)
     spans, steps = ranges([part[0].shape[1] for part in parts], tile)
     sub = count // row_count
     first = start // tile
@@ -260,7 +263,7 @@
             if not last:
                 outs[0][...] = acc_ref[...]
                 return
-            col, row = sc_ref[0], sc_ref[1]
+            col, row = sc_ref[2], sc_ref[3]
             for t in range(row_count):
                 at = pl.multiple_of((row ^ t) * sub, sub)
                 for p in range(panels):
@@ -300,24 +303,26 @@
     order = slots * wide
     tile = tile_of(size, 2048)
     sub_gram = order // row_count
+    needed = [(k, p) for k in range(slots) for p in range(panels) if k == 0 or p > 0]
 
     def kernel(sc_ref, *refs):
-        piece_refs, (gram_out, gram_ref, nat_ref) = refs[:slots], refs[slots:]
+        panel_refs = dict(zip(needed, refs))
+        gram_out, gram_ref, nat_ref = refs[len(needed) :]
         step = pl.program_id(0)
         for n, (later, earlier) in enumerate(pairs):
-            panel = jnp.concatenate([piece_refs[k][later] for k in range(slots)], axis=1)
+            panel = jnp.concatenate([panel_refs[k, later][0] for k in range(slots)], axis=1)
             product = lax.dot_general(
-                panel, piece_refs[0][earlier], TN, preferred_element_type=jnp.float32
+                panel_refs[0, earlier][0], panel, TN, preferred_element_type=jnp.float32
             )
             add_up(step, gram_ref.at[n], product)
 
         @pl.when(step == pl.num_programs(0) - 1)
         def _():
-            col, row = sc_ref[0], sc_ref[1]
+            col, row = sc_ref[2], sc_ref[3]
             for n in range(len(pairs)):
                 for k in range(slots):
                     at = pl.multiple_of((col ^ k) * wide, wide)
-                    nat_ref[pl.ds(at, wide), :] = gram_ref[n, k * wide : (k + 1) * wide, :]
+                    nat_ref[pl.ds(at, wide), :] = gram_ref[n, :, k * wide : (k + 1) * wide].T
                 for t in range(row_count):
                     at = pl.multiple_of((row ^ t) * sub_gram, sub_gram)
                     gram_out[t, n] = nat_ref[pl.ds(at, sub_gram), :].astype(jnp.bfloat16)
@@ -328,16 +333,16 @@
         grid_spec=pltpu.PrefetchScalarGridSpec(
             num_scalar_prefetch=1,
             grid=(size // tile,),
-            in_specs=[pl.BlockSpec((panels, tile, wide), lambda i, sc: (0, i, 0))] * slots,
+            in_specs=[pl.BlockSpec((1, tile, wide), lambda i, sc, p=p: (p, i, 0)) for _, p in needed],
             out_specs=pl.BlockSpec(out_shape.shape, lambda i, sc: (0, 0, 0, 0)),
             scratch_shapes=[
-                pltpu.VMEM((len(pairs), order, wide), jnp.float32),
+                pltpu.VMEM((len(pairs), wide, order), jnp.float32),
                 pltpu.VMEM((order, wide), jnp.float32),
             ],
         ),
         out_shape=out_shape,
         name="gram",
-    )(place, *pieces)
+    )(place, *(pieces[k] for k, _ in needed))
 
 
 def coefficients(place, shares, grams, triangles, pairs):
@@ -350,7 +355,7 @@
         share_refs = refs[: len(shares)]
         gram_refs = refs[len(shares) : len(shares) + slots]
         tri_ref, out_ref, nat_ref = refs[len(shares) + slots :]
-        col, row = sc_ref[0], sc_ref[1]
+        col, row = sc_ref[2], sc_ref[3]
         for n in range(len(pairs)):
             for k in range(slots):
                 for t in range(row_count):
@@ -396,7 +401,7 @@
     count = parts[0][0].shape[0]
     order = slots * wide
     leads = partial is None
-    tile = min([tile_of(part[2].shape[1], 1024) for part in parts])
+    tile = min([tile_of(part[2].shape[1], 2048) for part in parts])
     spans, steps = ranges([part[2].shape[1] for part in parts], tile)
     first = start // tile
     n_coef, n_scale = len(coefs), len(scales)
@@ -416,7 +421,7 @@
 
             @pl.when(step == 0)
             def _():
-                col, row = sc_ref[0], sc_ref[1]
+                col, row = sc_ref[2], sc_ref[3]
                 sub = coef_refs[0].shape[0]
                 for t in range(n_coef):
                     rows = pl.ds(pl.multiple_of((row ^ t) * sub, sub), sub)
@@ -530,51 +535,36 @@
         pieces[slow + fast] = swap(pieces[slow], "col", fast)
 
     first_column = row_index // half_rows * (order_size // 2) + col_index * col_width
-    place = jnp.stack([first_column, side_index])
-    here = jnp.stack([col_index, row_index])
+    slots = [k + f for f in range(1, slow) for k in (slow, 0)] + [slow, 0]
+    place = jnp.stack([first_column, side_index, col_index, row_index] + [col_index ^ k for k in slots])
     col_tables = column_tables(place, pole_order, pole_sq, coupling, deflated, col_width)
     tables = [x.reshape(order_size // LANES, LANES) for x in (pole_sq, deflated, pole_order)]
     anchors3 = anchors.reshape(col_count, 1, count)
     fraction3 = root_fraction.reshape(col_count, 1, count)
-    slots = [k + s for s in range(1, slow) for k in (slow, 0)] + [slow, 0]
-    mix, squares, dead = mixing_rows(place, col_index, slots, anchors3, fraction3, tables, col_tables)
+    mix, squares, dead = mixing_rows(place, slots, anchors3, fraction3, tables, col_tables)
     half_squares = squares[-1]
     for n, k in enumerate(slots[:-1]):
         half_squares = half_squares + swap(squares[n], "col", k)
     other_squares = swap(half_squares, "row", half_rows)
 
     size = old.shape[0]
-    chunk = size // 4
+    lengths = [size // 4, size // 2, size // 4]
+    starts = [sum(lengths[:n]) for n in range(3)]
     far, own, near = [], [], []
-    for n in range(4):
-        sent, keep_far, keep_own = merge(mix, old, n * chunk, chunk, (count, count))
+    for n in range(3):
+        sent, keep_far, keep_own = merge(mix, old, starts[n], lengths[n], (count, count))
         got = None
         for fast in range(1, slow):
             part = swap(sent[(fast - 1) * 2 * count : fast * 2 * count], "col", fast)
             got = part if got is None else got + part
-        far.append(keep_far)
+        far.append(keep_far + got[:count])
         own.append(keep_own)
         near.append(got)
-
-    def far_sum(n, lane, length):
-        lanes = slice(lane, lane + length)
-        return far[n][:, lanes] + near[n][:count, lanes]
-
-    gram = panel_products(here, pieces, row_count, pairs)
-    half = chunk // 2
-    spans = [(0, 0, chunk), (1, 0, chunk), (2, 0, half), (2, half, half), (3, 0, half), (3, half, half)]
-    whole_far = [far_sum(n, 0, chunk) for n in range(4)]
-    early = 3
-    cut = [whole_far[n] if length == chunk else whole_far[n][:, lane : lane + length] for n, lane, length in spans]
+    gram = panel_products(place, pieces, row_count, pairs)
     arrived = []
-    for n in range(early):
-        arrived.append(swap(cut[n], "col", slow))
-    (acc,) = project(
-        here, [(whole_far[n], own[n], near[n]) for n in range(3)], 0, pieces, row_count, None, False
-    )
-    far_proj, own_proj = project(
-        here, [(whole_far[3], own[3], near[3])], 3 * chunk, pieces, row_count, acc, True
-    )
+    for n in range(2):
+        arrived.append(swap(far[n], "col", slow))
+    far_proj, own_proj = project(place, list(zip(far, own, near)), 0, pieces, row_count)
 
     gram_sum = gram[0].astype(jnp.float32)
     far_total = far_proj[0].astype(jnp.float32)
@@ -586,29 +576,24 @@
     for t in range(1, row_count):
         shares.append(swap(own_proj[t], "row", t))
     gram_sum = gram_sum.astype(jnp.bfloat16)
-    gram_rows = jnp.stack([gram_sum] + [swap(gram_sum, "row", t) for t in range(1, row_count)])
+    gathered = [gram_sum]
+    for t in range(1, row_count):
+        gathered.append(swap(gram_sum, "row", t))
+    gram_rows = jnp.stack(gathered)
     grams = [None] * col_count
-    grams[0], grams[slow] = gram_rows, swap(gram_rows, "col", slow)
+    grams[0] = gram_rows
+    grams[slow] = swap(gram_rows, "col", slow)
     for fast in range(1, slow):
         grams[fast] = swap(gram_rows, "col", fast)
         grams[slow + fast] = swap(grams[slow], "col", fast)
     shares.append(swap(far_total, "col", slow))
-    for n in range(early, len(spans)):
-        arrived.append(swap(after(cut[n], far_total), "col", slow))
-    coef = coefficients(here, shares, grams, triangles[0], pairs)
+    arrived.append(swap(after(far[2], far_total), "col", slow))
+    coef = coefficients(place, shares, grams, triangles[0], pairs)
     coefs = [coef] + [swap(coef, "row", t) for t in range(1, row_count)]
 
-    def part_of(m):
-        n, lane, _ = spans[m]
-        return (own[n], near[n], arrived[m], lane)
-
-    starts = [n * chunk + lane for n, lane, _ in spans]
-    result, coef_all, scale_all = finish(
-        here, [part_of(m) for m in range(4)], 0, pieces, coefs, [half_squares, other_squares, dead[-1]]
-    )
-    for m in (4, 5):
-        (result,) = finish(here, [part_of(m)], starts[m], pieces, [coef_all], [scale_all], result)
-    return result[None]
+    parts = [(*part, 0) for part in zip(own, near, arrived)]
+    norms = [half_squares, other_squares, dead[-1]]
+    return finish(place, parts, 0, pieces, coefs, norms)[0][None]
 
 
 def solution(mesh):

time: 368 us -> 286 us (0.78)
  waiting for transfers between devices: 127 us -> 82.5 us
  Pallas kernels: 177 us -> 150 us
  starting transfers between devices: 43.1 us -> 35.5 us
  other arithmetic: 11.6 us -> 7.25 us
    ppermute x36 -> x32, waiting for transfers between devices: 127 us -> 82.5 us  [swap(): return lax.ppermute(x, axis, [(i, i ^ mask) for i in range(size)])]
    pallas_call x4 -> x3, Pallas kernels: 95 us -> 83.9 us  [merge(): pl.pallas_call(kernel, grid=(size // rows,), in_specs=[pl.BlockSpec((tota...]
    ppermute x36 -> x32, starting transfers between devices: 43.1 us -> 35.5 us  [swap(): return lax.ppermute(x, axis, [(i, i ^ mask) for i in range(size)])]
    pallas_call x3 -> x1, Pallas kernels: 21.5 us -> 15 us  [finish(): pl.pallas_call(kernel, grid_spec=pltpu.PrefetchScalarGridSpec(num_scalar_...]
    pallas_call x2 -> x1, Pallas kernels: 23.7 us -> 18 us  [project(): pl.pallas_call(kernel, grid_spec=pltpu.PrefetchScalarGridSpec(num_scalar_...]
  transfers between devices with their start and end apart: 36 -> 32, of which waited for: 13 -> 14; matrix products, arithmetic and copies ran while one was open for 5% -> 5% of each run, Pallas kernels for 47% -> 47%
where the time goes in v2:
time: 286 us; the launch traced here: 285 us
  Pallas kernels  150 us (52%)
  waiting for transfers between devices  82.5 us (29%)
  starting transfers between devices  35.5 us (12%)
  local copies, waits for them, and re-layouts  9.45 us (3%)
  other arithmetic  7.25 us (3%)
    pallas_call x3, Pallas kernels, merge(): pl.pallas_call(kernel, grid=(size // rows,), in_specs=[pl.BlockSpec((tota...  83.9 us
    ppermute x32, waiting for transfers between devices, swap(): return lax.ppermute(x, axis, [(i, i ^ mask) for i in range(size)])  82.5 us
    ppermute x32, starting transfers between devices, swap(): return lax.ppermute(x, axis, [(i, i ^ mask) for i in range(size)])  35.5 us
    pallas_call x1, Pallas kernels, project(): pl.pallas_call(kernel, grid_spec=pltpu.PrefetchScalarGridSpec(num_scalar_...  18 us
    pallas_call x1, Pallas kernels, mixing_rows(): pl.pallas_call(mixing_kernel, grid_spec=pltpu.PrefetchScalarGridSpec(num_...  15.1 us
    pallas_call x1, Pallas kernels, finish(): pl.pallas_call(kernel, grid_spec=pltpu.PrefetchScalarGridSpec(num_scalar_...  15 us
    pallas_call x1, Pallas kernels, panel_products(): pl.pallas_call(kernel, grid_spec=pltpu.PrefetchScalarGridSpec(num_scalar_...  6.81 us
    pallas_call x1, Pallas kernels, column_tables(): pl.pallas_call(column_kernel, grid_spec=pltpu.PrefetchScalarGridSpec(num_...  5.9 us
  transfers between devices with their start and end apart: 32, of which 14 were waited for; matrix products, arithmetic and copies ran while one was open for 5% of the time, Pallas kernels for 47%

profile of v2, /device:TPU:0, one launch (start us, length us, event | category | flops | bytes accessed | tf_op | source)
XLA Modules:
  0.0 285.4 jit_solution(4917735872234709729)
XLA Ops:
  0.0 3.0 %collective-permute-start.6 = (bf16[2,8192,128]{2,1,0:T(8,128)(2,1)}, bf16[2,8192,128]{2,1,0:T(8,128)(2,1)}, u32[]{:S(2)}, u32[]{:S(2)}) collective-permute-start(bf16[2,8192,128]{2,1,0:T(8,128)(2,1)} %bitcast.68), channel_id=1, source_target_pairs={{0,2},{1,3},{2,0},{3,1},{4,6},{5,7},{6,4},{7,5},{8,10},{9,11},{10,... | collective-permute-start | bytes 12582920 | tf_op jit(solution)/shard_map/ppermute | solution.py:529
  3.0 0.7 stack.47.place_ref.sc_ref
  3.7 5.9 %columns.1 = (f32[32,128]{1,0:T(8,128)}, f32[32,128]{1,0:T(8,128)}) custom-call(s32[8]{0:T(128)} %stack.47.place_ref.sc_ref, s32[1,32768]{1,0:T(1,128)} %bitcast.79, f32[1,32768]{1,0:T(1,128)} %bitcast.75, f32[1,32768]{1,0:T(1,128)} %bitcast.81, s32[1,32768]{1,0:T(1,128)} %bitcast.77), custom_call_target="tpu_custom_call" | custom-call | tf_op jit(solution)/shard_map/columns/pallas_call | solution.py:83
  9.6 15.1 %mixing.1 = (bf16[1024,4096]{1,0:T(8,128)(2,1)}, f32[4,1,256]{2,1,0:T(1,128)}, f32[4,1,256]{2,1,0:T(1,128)}) custom-call(s32[8]{0:T(128)} %stack.47.place_ref.sc_ref, s32[4,1,256]{2,1,0:T(1,128)} %bitcast.86, f32[4,1,256]{2,1,0:T(1,128)} %bitcast.87, f32[256,128]{1,0:T(8,128)} %bitcast.76, s32[256,128]{1,0:T(8,128)} %bitcast.78, s32[256,128]{1,0:T(8,128)} %bitcast.80, ...), custom_call_target="tpu_custom_call" | custom-call | tf_op jit(solution)/shard_map/mixing/pallas_call | solution.py:168
  24.7 42.0 %merge.4 = (bf16[512,4096]{1,0:T(8,128)(2,1)}, bf16[256,4096]{1,0:T(8,128)(2,1)S(1)}, bf16[256,4096]{1,0:T(8,128)(2,1)S(1)}) custom-call(bf16[1024,4096]{1,0:T(8,128)(2,1)} %get-tuple-element.25.mix_ref, bf16[8192,4096]{1,0:T(8,128)(2,1)} %bitcast.16.old_ref), custom_call_target="tpu_custom_call" | custom-call | tf_op jit(solution)/shard_map/merge/pallas_call | solution.py:197
  66.7 21.4 %merge.3 = (bf16[512,2048]{1,0:T(8,128)(2,1)S(1)}, bf16[256,2048]{1,0:T(8,128)(2,1)S(1)}, bf16[256,2048]{1,0:T(8,128)(2,1)S(1)}) custom-call(bf16[1024,4096]{1,0:T(8,128)(2,1)S(1)} %bitcast.67, bf16[8192,4096]{1,0:T(8,128)(2,1)} %bitcast.16.old_ref), custom_call_target="tpu_custom_call" | custom-call | tf_op jit(solution)/shard_map/merge/pallas_call | solution.py:197
  88.1 1.0 copy-done.1
  89.0 0.5 collective-permute-start
  89.6 0.1 collective-permute-start.5
  89.6 4.2 %collective-permute-done.6.refs_11_.refs_3_ = bf16[2,8192,128]{2,1,0:T(8,128)(2,1)} collective-permute-done((bf16[2,8192,128]{2,1,0:T(8,128)(2,1)}, bf16[2,8192,128]{2,1,0:T(8,128)(2,1)}, u32[]{:S(2)}, u32[]{:S(2)}) %collective-permute-start.6) | collective-permute-done | bytes 4194336 | tf_op jit(solution)/shard_map/ppermute | solution.py:529
  93.9 20.6 %merge.5 = (bf16[512,2048]{1,0:T(8,128)(2,1)S(1)}, bf16[256,2048]{1,0:T(8,128)(2,1)S(1)}, bf16[256,2048]{1,0:T(8,128)(2,1)S(1)}) custom-call(bf16[1024,4096]{1,0:T(8,128)(2,1)S(1)} %bitcast.67, bf16[8192,4096]{1,0:T(8,128)(2,1)} %bitcast.16.old_ref), custom_call_target="tpu_custom_call" | custom-call | tf_op jit(solution)/shard_map/merge/pallas_call | solution.py:197
  114.5 0.6 collective-permute-start.4
  115.1 0.5 slice_bitcast_fusion.14
  115.6 1.7 collective-permute-start.30
  117.3 1.1 slice_add_fusion.2.refs_0_
  118.5 3.1 %slice_add_fusion.refs_3_ = bf16[256,4096]{1,0:T(8,128)(2,1)} fusion(bf16[256,4096]{1,0:T(8,128)(2,1)S(1)} %get-tuple-element.31, bf16[512,4096]{1,0:T(8,128)(2,1)} %collective-permute-done.2.refs_5_.refs_4_), kind=kLoop, calls=%fused_computation | loop fusion | flops 1048576 | bytes 6291456 | tf_op jit(solution)/shard_map/add | solution.py:560
  121.6 0.5 collective-permute-start.3
  122.1 1.2 slice_add_fusion.1.refs_6_
  123.3 0.5 copy-done.5
  123.8 18.0 %project.1 = (bf16[4,64,1024]{2,1,0:T(8,128)(2,1)}, bf16[4,64,1024]{2,1,0:T(8,128)(2,1)}) custom-call(s32[8]{0:T(128)} %stack.47.place_ref.sc_ref, bf16[256,2048]{1,0:T(8,128)(2,1)} %slice_add_fusion.2.refs_0_, bf16[256,2048]{1,0:T(8,128)(2,1)} %copy-done.1, bf16[512,2048]{1,0:T(8,128)(2,1)} %copy-done.4, bf16[256,4096]{1,0:T(8,128)(2,1)} %slice_add_fusion.refs_3_, ...), custom_call_target="tpu_custom_call" | custom-call | tf_op jit(solution)/shard_map/project/pallas_call | solution.py:287
  141.8 1.7 slice_bitcast_fusion.6
  143.5 3.6 %collective-permute-start.10 = (bf16[64,1024]{1,0:T(8,128)(2,1)S(1)}, bf16[64,1024]{1,0:T(8,128)(2,1)S(1)}, u32[]{:S(2)}, u32[]{:S(2)}) collective-permute-start(bf16[64,1024]{1,0:T(8,128)(2,1)S(1)} %get-tuple-element.46), channel_id=1, source_target_pairs={{0,12},{4,8},{8,4},{12,0},{1,13},{5,9},{9,5},{13,1},{2,14},{6,10},... | collective-permute-start | bytes 393224 | tf_op jit(solution)/shard_map/ppermute | solution.py:529
  147.1 0.8 collective-permute-start.8
  147.9 6.8 %gram.1 = bf16[4,1,128,128]{3,2,1,0:T(8,128)(2,1)} custom-call(s32[8]{0:T(128)} %stack.47.place_ref.sc_ref, bf16[2,8192,128]{2,1,0:T(8,128)(2,1)} %bitcast.70, bf16[2,8192,128]{2,1,0:T(8,128)(2,1)} %bitcast.71, bf16[2,8192,128]{2,1,0:T(8,128)(2,1)} %collective-permute-done.5.refs_10_.refs_2_, bf16[2,8192,128]{2,1,0:T(8,128)(2,1)} %collective-permute-done.6.refs_11_.refs_3_, ...), custom_call_target="tpu_custom_call" | custom-call | tf_op jit(solution)/shard_map/gram/pallas_call | solution.py:331
  154.7 0.8 slice_bitcast_fusion.9
  155.5 0.1 collective-permute-start.29
  155.6 2.5 collective-permute-done.9
  158.1 1.3 collective-permute-start.1
  159.4 2.5 collective-permute-start.18
  161.9 1.0 fusion.2
  162.9 0.1 collective-permute-start.17
  163.0 1.9 collective-permute-start.16
  164.9 0.3 collective-permute-done.18
  165.1 0.7 collective-permute-start.11
  165.8 1.8 slice_bitcast_fusion
  167.6 0.1 collective-permute-done.17
  167.7 1.0 collective-permute-start.12
  168.8 0.8 fusion.5
  169.5 43.4 %collective-permute-done.28 = f32[1,256]{1,0:T(1,128)S(1)} collective-permute-done((f32[1,256]{1,0:T(1,128)S(1)}, f32[1,256]{1,0:T(1,128)S(1)}, u32[]{:S(2)}, u32[]{:S(2)}) %collective-permute-start.28) | collective-permute-done | bytes 1056 | tf_op jit(solution)/shard_map/ppermute | solution.py:529
  213.0 3.6 %collective-permute-start.21 = (bf16[1,128,128]{2,1,0:T(8,128)(2,1)S(1)}, bf16[1,128,128]{2,1,0:T(8,128)(2,1)S(1)}, u32[]{:S(2)}, u32[]{:S(2)}) collective-permute-start(bf16[1,128,128]{2,1,0:T(8,128)(2,1)S(1)} %fusion.5), channel_id=1, source_target_pairs={{0,12},{4,8},{8,4},{12,0},{1,13},{5,9},{9,5},{13,1},{2,14},{6,10},... | collective-permute-start | bytes 98312 | tf_op jit(solution)/shard_map/ppermute | solution.py:529
  216.6 2.1 collective-permute-done.21
  218.7 0.8 collective-permute-start.20
  219.5 4.7 %collective-permute-done.20 = bf16[1,128,128]{2,1,0:T(8,128)(2,1)S(1)} collective-permute-done((bf16[1,128,128]{2,1,0:T(8,128)(2,1)S(1)}, bf16[1,128,128]{2,1,0:T(8,128)(2,1)S(1)}, u32[]{:S(2)}, u32[]{:S(2)}) %collective-permute-start.20) | collective-permute-done | bytes 32800 | tf_op jit(solution)/shard_map/ppermute | solution.py:529
  224.2 0.5 collective-permute-start.19
  224.8 3.4 %collective-permute-done.19 = bf16[1,128,128]{2,1,0:T(8,128)(2,1)S(1)} collective-permute-done((bf16[1,128,128]{2,1,0:T(8,128)(2,1)S(1)}, bf16[1,128,128]{2,1,0:T(8,128)(2,1)S(1)}, u32[]{:S(2)}, u32[]{:S(2)}) %collective-permute-start.19) | collective-permute-done | bytes 32800 | tf_op jit(solution)/shard_map/ppermute | solution.py:529
  228.1 1.4 collective-permute-start.13
  229.6 1.5 collective-permute-start.14
  231.1 7.6 %collective-permute-done.13.refs_2_ = bf16[64,1024]{1,0:T(8,128)(2,1)S(1)} collective-permute-done((bf16[64,1024]{1,0:T(8,128)(2,1)S(1)}, bf16[64,1024]{1,0:T(8,128)(2,1)S(1)}, u32[]{:S(2)}, u32[]{:S(2)}) %collective-permute-start.13) | collective-permute-done | bytes 131104 | tf_op jit(solution)/shard_map/ppermute | solution.py:529
  238.7 0.8 collective-permute-start.23
  239.5 0.6 collective-permute-done.22.refs_6_
  240.1 0.8 collective-permute-start.15
  240.8 4.3 %collective-permute-done.23.refs_7_ = bf16[4,1,128,128]{3,2,1,0:T(8,128)(2,1)S(1)} collective-permute-done((bf16[4,1,128,128]{3,2,1,0:T(8,128)(2,1)S(1)}, bf16[4,1,128,128]{3,2,1,0:T(8,128)(2,1)S(1)}, u32[]{:S(2)}, u32[]{:S(2)}) %collective-permute-start.23) | collective-permute-done | bytes 131104 | tf_op jit(solution)/shard_map/ppermute | solution.py:529
  245.2 2.2 collective-permute-done.15.refs_4_
  247.4 3.3 %collective-permute-start.31 = (f32[1,256]{1,0:T(1,128)S(1)}, f32[1,256]{1,0:T(1,128)S(1)}, u32[]{:S(2)}, u32[]{:S(2)}) collective-permute-start(f32[1,256]{1,0:T(1,128)S(1)} %fusion.7.refs_17_), channel_id=1, source_target_pairs={{0,8},{4,12},{8,0},{12,4},{1,9},{5,13},{9,1},{13,5},{2,10},{6,14},... | collective-permute-start | bytes 3080 | tf_op jit(solution)/shard_map/ppermute | solution.py:529
  250.7 0.6 copy-done.19
  251.4 5.6 %coefficients.1.refs_13_ = bf16[64,1024]{1,0:T(8,128)(2,1)} custom-call(s32[8]{0:T(128)} %stack.47.place_ref.sc_ref, bf16[64,1024]{1,0:T(8,128)(2,1)} %get-tuple-element.44.refs_0_, bf16[64,1024]{1,0:T(8,128)(2,1)} %copy-done.13, bf16[64,1024]{1,0:T(8,128)(2,1)} %copy-done.14, bf16[64,1024]{1,0:T(8,128)(2,1)} %copy-done.15, bf16[64,1024]{1,0:T(8,128)(2,1)} %copy-done.18, ...), custom_call_target="tpu_custom_call" | custom-call | tf_op jit(solution)/shard_map/coefficients/pallas_call | solution.py:385
  257.0 1.0 collective-permute-start.26
  258.0 3.4 %collective-permute-start.27 = (bf16[64,1024]{1,0:T(8,128)(2,1)}, bf16[64,1024]{1,0:T(8,128)(2,1)S(1)}, u32[]{:S(2)}, u32[]{:S(2)}) collective-permute-start(bf16[64,1024]{1,0:T(8,128)(2,1)} %coefficients.1.refs_13_), channel_id=1, source_target_pairs={{0,12},{4,8},{8,4},{12,0},{1,13},{5,9},{9,5},{13,1},{2,14},{6,10},... | collective-permute-start | bytes 393224 | tf_op jit(solution)/shard_map/ppermute | solution.py:529
  261.4 1.2 slice_bitcast_fusion.11.refs_19_
  262.6 0.6 collective-permute-done.25.refs_14_
  263.1 6.4 %collective-permute-done.26.refs_15_ = bf16[64,1024]{1,0:T(8,128)(2,1)S(1)} collective-permute-done((bf16[64,1024]{1,0:T(8,128)(2,1)}, bf16[64,1024]{1,0:T(8,128)(2,1)S(1)}, u32[]{:S(2)}, u32[]{:S(2)}) %collective-permute-start.26) | collective-permute-done | bytes 131104 | tf_op jit(solution)/shard_map/ppermute | solution.py:529
  269.6 0.6 copy-done.11
  270.2 0.0 copy-done.12
  270.2 15.0 %finish.1 = (bf16[256,8192]{1,0:T(8,128)(2,1)}, bf16[256,1024]{1,0:T(8,128)(2,1)}, f32[256,128]{1,0:T(8,128)}) custom-call(s32[8]{0:T(128)} %stack.47.place_ref.sc_ref, bf16[256,2048]{1,0:T(8,128)(2,1)} %copy-done.1, bf16[512,2048]{1,0:T(8,128)(2,1)} %copy-done.4, bf16[256,2048]{1,0:T(8,128)(2,1)} %copy-done.8, bf16[256,4096]{1,0:T(8,128)(2,1)} %copy-done, ...), custom_call_target="tpu_custom_call" | custom-call | tf_op jit(solution)/shard_map/finish/pallas_call | solution.py:484
  (73 shorter events, 0.2 us)
Async XLA Ops:
  0.0 93.9 %collective-permute-start.6 = (bf16[2,8192,128]{2,1,0:T(8,128)(2,1)}, bf16[2,8192,128]{2,1,0:T(8,128)(2,1)}, u32[]{:S(2)}, u32[]{:S(2)}) collective-permute-start(bf16[2,8192,128]{2,1,0:T(8,128)(2,1)} %bitcast.68), channel_id=1, source_target_pairs={{0,2},{1,3},{2,0},{3,1},{4,6},{5,7},{6,4},{7,5},{8,10},{9,11},{10,... | collective-permute-start | bytes 12582920 | tf_op jit(solution)/shard_map/ppermute | solution.py:529
  24.6 42.0 %slice-start = ((s8[8388608]{0:T(1024)(128)(4,1)}), s8[4194304]{0:T(1024)(128)(4,1)S(1)}, s32[]{:S(2)}) async-start(s8[8388608]{0:T(1024)(128)(4,1)} %bitcast.66), calls=%async_computation | async-start | bytes 8388608
  24.6 42.0 %slice-start.1 = ((s8[8388608]{0:T(1024)(128)(4,1)}), s8[4194304]{0:T(1024)(128)(4,1)S(1)}, s32[]{:S(2)}) async-start(s8[8388608]{0:T(1024)(128)(4,1)} %bitcast.66), calls=%async_computation.1 | async-start | bytes 8388608
  66.6 21.4 %copy-start = (bf16[256,4096]{1,0:T(8,128)(2,1)}, bf16[256,4096]{1,0:T(8,128)(2,1)S(1)}, u32[]{:S(2)}) copy-start(bf16[256,4096]{1,0:T(8,128)(2,1)S(1)} %get-tuple-element.29.refs_4_.refs_3_) | copy-start | bytes 6291460
  66.6 22.9 %copy-start.3 = (bf16[1,2,8192,128]{3,2,1,0:T(8,128)(2,1)S(1)}, bf16[1,2,8192,128]{3,2,1,0:T(8,128)(2,1)}, u32[]{:S(2)}) copy-start(bf16[1,2,8192,128]{3,2,1,0:T(8,128)(2,1)} %param.10) | copy-start | bytes 12582916
  66.6 51.8 %collective-permute-start.2 = (bf16[512,4096]{1,0:T(8,128)(2,1)}, bf16[512,4096]{1,0:T(8,128)(2,1)}, u32[]{:S(2)}, u32[]{:S(2)}) collective-permute-start(bf16[512,4096]{1,0:T(8,128)(2,1)} %get-tuple-element.30), channel_id=1, source_target_pairs={{0,1},{1,0},{2,3},{3,2},{4,5},{5,4},{6,7},{7,6},{8,9},{9,8},{10,11... | collective-permute-start | bytes 12582920 | tf_op jit(solution)/shard_map/ppermute | solution.py:529
  88.1 1.0 copy-start.1
  89.0 26.0 %copy-start.21 = (f32[4,1,256]{2,1,0:T(1,128)S(1)}, f32[4,1,256]{2,1,0:T(1,128)}, u32[]{:S(2)}) copy-start(f32[4,1,256]{2,1,0:T(1,128)} %get-tuple-element.38) | copy-start | bytes 12292
  89.0 26.6 %collective-permute-start = (bf16[512,2048]{1,0:T(8,128)(2,1)S(1)}, bf16[512,2048]{1,0:T(8,128)(2,1)S(1)}, u32[]{:S(2)}, u32[]{:S(2)}) collective-permute-start(bf16[512,2048]{1,0:T(8,128)(2,1)S(1)} %get-tuple-element.27), channel_id=1, source_target_pairs={{0,1},{1,0},{2,3},{3,2},{4,5},{5,4},{6,7},{7,6},{8,9},{9,8},{10,11... | collective-permute-start | bytes 6291464 | tf_op jit(solution)/shard_map/ppermute | solution.py:529
  89.6 33.8 %collective-permute-start.5 = (bf16[2,8192,128]{2,1,0:T(8,128)(2,1)S(1)}, bf16[2,8192,128]{2,1,0:T(8,128)(2,1)}, u32[]{:S(2)}, u32[]{:S(2)}) collective-permute-start(bf16[2,8192,128]{2,1,0:T(8,128)(2,1)S(1)} %bitcast.73), channel_id=1, source_target_pairs={{0,1},{1,0},{2,3},{3,2},{4,5},{5,4},{6,7},{7,6},{8,9},{9,8},{10,11... | collective-permute-start | bytes 12582920 | tf_op jit(solution)/shard_map/ppermute | solution.py:529
  93.9 29.9 %collective-permute-start.7 = (bf16[2,8192,128]{2,1,0:T(8,128)(2,1)}, bf16[2,8192,128]{2,1,0:T(8,128)(2,1)}, u32[]{:S(2)}, u32[]{:S(2)}) collective-permute-start(bf16[2,8192,128]{2,1,0:T(8,128)(2,1)} %collective-permute-done.6.refs_11_.refs_3_), channel_id=1, source_target_pairs={{0,1},{1,0},{2,3},{3,2},{4,5},{5,4},{6,7},{7,6},{8,9},{9,8},{10,11... | collective-permute-start | bytes 12582920 | tf_op jit(solution)/shard_map/ppermute | solution.py:529
  114.5 7.1 %copy-start.2 = (bf16[256,2048]{1,0:T(8,128)(2,1)}, bf16[256,2048]{1,0:T(8,128)(2,1)S(1)}, u32[]{:S(2)}) copy-start(bf16[256,2048]{1,0:T(8,128)(2,1)S(1)} %get-tuple-element.32.refs_7_.refs_6_) | copy-start | bytes 3145732
  114.5 7.6 %collective-permute-start.4 = (bf16[512,2048]{1,0:T(8,128)(2,1)S(1)}, bf16[512,2048]{1,0:T(8,128)(2,1)S(1)}, u32[]{:S(2)}, u32[]{:S(2)}) collective-permute-start(bf16[512,2048]{1,0:T(8,128)(2,1)S(1)} %get-tuple-element.33), channel_id=1, source_target_pairs={{0,1},{1,0},{2,3},{3,2},{4,5},{5,4},{6,7},{7,6},{8,9},{9,8},{10,11... | collective-permute-start | bytes 6291464 | tf_op jit(solution)/shard_map/ppermute | solution.py:529
  115.6 6.0 %copy-start.4 = (bf16[512,2048]{1,0:T(8,128)(2,1)}, bf16[512,2048]{1,0:T(8,128)(2,1)S(1)}, u32[]{:S(2)}) copy-start(bf16[512,2048]{1,0:T(8,128)(2,1)S(1)} %collective-permute-done.refs_2_.refs_1_) | copy-start | bytes 6291460
  115.6 47.3 %collective-permute-start.30 = (f32[1,256]{1,0:T(1,128)}, f32[1,256]{1,0:T(1,128)S(1)}, u32[]{:S(2)}, u32[]{:S(2)}) collective-permute-start(f32[1,256]{1,0:T(1,128)} %get-tuple-element.52), channel_id=1, source_target_pairs={{0,2},{1,3},{2,0},{3,1},{4,6},{5,7},{6,4},{7,5},{8,10},{9,11},{10,... | collective-permute-start | bytes 3080 | tf_op jit(solution)/shard_map/ppermute | solution.py:529
  121.6 141.0 %collective-permute-start.3 = (bf16[256,4096]{1,0:T(8,128)(2,1)}, bf16[256,4096]{1,0:T(8,128)(2,1)}, u32[]{:S(2)}, u32[]{:S(2)}) collective-permute-start(bf16[256,4096]{1,0:T(8,128)(2,1)} %slice_add_fusion.refs_3_), channel_id=1, source_target_pairs={{0,2},{1,3},{2,0},{3,1},{4,6},{5,7},{6,4},{7,5},{8,10},{9,11},{10,... | collective-permute-start | bytes 6291464 | tf_op jit(solution)/shard_map/ppermute | solution.py:529
  122.1 1.7 copy-start.5
  143.5 12.0 %collective-permute-start.10 = (bf16[64,1024]{1,0:T(8,128)(2,1)S(1)}, bf16[64,1024]{1,0:T(8,128)(2,1)S(1)}, u32[]{:S(2)}, u32[]{:S(2)}) collective-permute-start(bf16[64,1024]{1,0:T(8,128)(2,1)S(1)} %get-tuple-element.46), channel_id=1, source_target_pairs={{0,12},{4,8},{8,4},{12,0},{1,13},{5,9},{9,5},{13,1},{2,14},{6,10},... | collective-permute-start | bytes 393224 | tf_op jit(solution)/shard_map/ppermute | solution.py:529
  147.1 10.9 %collective-permute-start.9 = (bf16[64,1024]{1,0:T(8,128)(2,1)S(1)}, bf16[64,1024]{1,0:T(8,128)(2,1)S(1)}, u32[]{:S(2)}, u32[]{:S(2)}) collective-permute-start(bf16[64,1024]{1,0:T(8,128)(2,1)S(1)} %get-tuple-element.47), channel_id=1, source_target_pairs={{0,8},{4,12},{8,0},{12,4},{1,9},{5,13},{9,1},{13,5},{2,10},{6,14},... | collective-permute-start | bytes 393224 | tf_op jit(solution)/shard_map/ppermute | solution.py:529
  147.1 10.9 %copy-start.7 = (bf16[256,2048]{1,0:T(8,128)(2,1)S(1)}, bf16[256,2048]{1,0:T(8,128)(2,1)}, u32[]{:S(2)}) copy-start(bf16[256,2048]{1,0:T(8,128)(2,1)} %slice_add_fusion.2.refs_0_) | copy-start | bytes 3145732
  147.1 18.0 %copy-start.6 = (bf16[256,2048]{1,0:T(8,128)(2,1)S(1)}, bf16[256,2048]{1,0:T(8,128)(2,1)}, u32[]{:S(2)}) copy-start(bf16[256,2048]{1,0:T(8,128)(2,1)} %slice_add_fusion.1.refs_6_) | copy-start | bytes 3145732
  147.1 12.3 %collective-permute-start.8 = (bf16[64,1024]{1,0:T(8,128)(2,1)}, bf16[64,1024]{1,0:T(8,128)(2,1)S(1)}, u32[]{:S(2)}, u32[]{:S(2)}) collective-permute-start(bf16[64,1024]{1,0:T(8,128)(2,1)} %get-tuple-element.45), channel_id=1, source_target_pairs={{0,4},{4,0},{8,12},{12,8},{1,5},{5,1},{9,13},{13,9},{2,6},{6,2},{1... | collective-permute-start | bytes 393224 | tf_op jit(solution)/shard_map/ppermute | solution.py:529
  155.5 7.4 %collective-permute-start.29 = (f32[1,256]{1,0:T(1,128)S(1)}, f32[1,256]{1,0:T(1,128)S(1)}, u32[]{:S(2)}, u32[]{:S(2)}) collective-permute-start(f32[1,256]{1,0:T(1,128)S(1)} %get-tuple-element.53), channel_id=1, source_target_pairs={{0,1},{1,0},{2,3},{3,2},{4,5},{5,4},{6,7},{7,6},{8,9},{9,8},{10,11... | collective-permute-start | bytes 3080 | tf_op jit(solution)/shard_map/ppermute | solution.py:529
  158.1 99.9 %collective-permute-start.1 = (bf16[256,2048]{1,0:T(8,128)(2,1)S(1)}, bf16[256,2048]{1,0:T(8,128)(2,1)S(1)}, u32[]{:S(2)}, u32[]{:S(2)}) collective-permute-start(bf16[256,2048]{1,0:T(8,128)(2,1)S(1)} %copy-done.7), channel_id=1, source_target_pairs={{0,2},{1,3},{2,0},{3,1},{4,6},{5,7},{6,4},{7,5},{8,10},{9,11},{10,... | collective-permute-start | bytes 3145736 | tf_op jit(solution)/shard_map/ppermute | solution.py:529
  159.4 5.7 %collective-permute-start.18 = (bf16[1,128,128]{2,1,0:T(8,128)(2,1)S(1)}, bf16[1,128,128]{2,1,0:T(8,128)(2,1)S(1)}, u32[]{:S(2)}, u32[]{:S(2)}) collective-permute-start(bf16[1,128,128]{2,1,0:T(8,128)(2,1)S(1)} %get-tuple-element.49), channel_id=1, source_target_pairs={{0,12},{4,8},{8,4},{12,0},{1,13},{5,9},{9,5},{13,1},{2,14},{6,10},... | collective-permute-start | bytes 98312 | tf_op jit(solution)/shard_map/ppermute | solution.py:529
  162.9 4.9 %collective-permute-start.17 = (bf16[1,128,128]{2,1,0:T(8,128)(2,1)S(1)}, bf16[1,128,128]{2,1,0:T(8,128)(2,1)S(1)}, u32[]{:S(2)}, u32[]{:S(2)}) collective-permute-start(bf16[1,128,128]{2,1,0:T(8,128)(2,1)S(1)} %get-tuple-element.50), channel_id=1, source_target_pairs={{0,8},{4,12},{8,0},{12,4},{1,9},{5,13},{9,1},{13,5},{2,10},{6,14},... | collective-permute-start | bytes 98312 | tf_op jit(solution)/shard_map/ppermute | solution.py:529
  163.0 4.8 %collective-permute-start.16 = (bf16[1,128,128]{2,1,0:T(8,128)(2,1)S(1)}, bf16[1,128,128]{2,1,0:T(8,128)(2,1)S(1)}, u32[]{:S(2)}, u32[]{:S(2)}) collective-permute-start(bf16[1,128,128]{2,1,0:T(8,128)(2,1)S(1)} %get-tuple-element.48), channel_id=1, source_target_pairs={{0,4},{4,0},{8,12},{12,8},{1,5},{5,1},{9,13},{13,9},{2,6},{6,2},{1... | collective-permute-start | bytes 98312 | tf_op jit(solution)/shard_map/ppermute | solution.py:529
  165.1 104.4 %collective-permute-start.11 = (bf16[256,2048]{1,0:T(8,128)(2,1)S(1)}, bf16[256,2048]{1,0:T(8,128)(2,1)}, u32[]{:S(2)}, u32[]{:S(2)}) collective-permute-start(bf16[256,2048]{1,0:T(8,128)(2,1)S(1)} %copy-done.6), channel_id=1, source_target_pairs={{0,2},{1,3},{2,0},{3,1},{4,6},{5,7},{6,4},{7,5},{8,10},{9,11},{10,... | collective-permute-start | bytes 3145736 | tf_op jit(solution)/shard_map/ppermute | solution.py:529
  167.7 45.2 %collective-permute-start.28 = (f32[1,256]{1,0:T(1,128)S(1)}, f32[1,256]{1,0:T(1,128)S(1)}, u32[]{:S(2)}, u32[]{:S(2)}) collective-permute-start(f32[1,256]{1,0:T(1,128)S(1)} %get-tuple-element.51), channel_id=1, source_target_pairs={{0,3},{1,2},{2,1},{3,0},{4,7},{5,6},{6,5},{7,4},{8,11},{9,10},{10,... | collective-permute-start | bytes 3080 | tf_op jit(solution)/shard_map/ppermute | solution.py:529
  167.7 61.8 %collective-permute-start.12 = (bf16[64,1024]{1,0:T(8,128)(2,1)S(1)}, bf16[64,1024]{1,0:T(8,128)(2,1)S(1)}, u32[]{:S(2)}, u32[]{:S(2)}) collective-permute-start(bf16[64,1024]{1,0:T(8,128)(2,1)S(1)} %get-tuple-element.43), channel_id=1, source_target_pairs={{0,4},{4,0},{8,12},{12,8},{1,5},{5,1},{9,13},{13,9},{2,6},{6,2},{1... | collective-permute-start | bytes 393224 | tf_op jit(solution)/shard_map/ppermute | solution.py:529
  213.0 5.7 %collective-permute-start.21 = (bf16[1,128,128]{2,1,0:T(8,128)(2,1)S(1)}, bf16[1,128,128]{2,1,0:T(8,128)(2,1)S(1)}, u32[]{:S(2)}, u32[]{:S(2)}) collective-permute-start(bf16[1,128,128]{2,1,0:T(8,128)(2,1)S(1)} %fusion.5), channel_id=1, source_target_pairs={{0,12},{4,8},{8,4},{12,0},{1,13},{5,9},{9,5},{13,1},{2,14},{6,10},... | collective-permute-start | bytes 98312 | tf_op jit(solution)/shard_map/ppermute | solution.py:529
  218.7 5.5 %collective-permute-start.20 = (bf16[1,128,128]{2,1,0:T(8,128)(2,1)S(1)}, bf16[1,128,128]{2,1,0:T(8,128)(2,1)S(1)}, u32[]{:S(2)}, u32[]{:S(2)}) collective-permute-start(bf16[1,128,128]{2,1,0:T(8,128)(2,1)S(1)} %fusion.5), channel_id=1, source_target_pairs={{0,8},{4,12},{8,0},{12,4},{1,9},{5,13},{9,1},{13,5},{2,10},{6,14},... | collective-permute-start | bytes 98312 | tf_op jit(solution)/shard_map/ppermute | solution.py:529
  224.2 3.9 %collective-permute-start.19 = (bf16[1,128,128]{2,1,0:T(8,128)(2,1)S(1)}, bf16[1,128,128]{2,1,0:T(8,128)(2,1)S(1)}, u32[]{:S(2)}, u32[]{:S(2)}) collective-permute-start(bf16[1,128,128]{2,1,0:T(8,128)(2,1)S(1)} %fusion.5), channel_id=1, source_target_pairs={{0,4},{4,0},{8,12},{12,8},{1,5},{5,1},{9,13},{13,9},{2,6},{6,2},{1... | collective-permute-start | bytes 98312 | tf_op jit(solution)/shard_map/ppermute | solution.py:529
  228.1 10.6 %collective-permute-start.13 = (bf16[64,1024]{1,0:T(8,128)(2,1)S(1)}, bf16[64,1024]{1,0:T(8,128)(2,1)S(1)}, u32[]{:S(2)}, u32[]{:S(2)}) collective-permute-start(bf16[64,1024]{1,0:T(8,128)(2,1)S(1)} %get-tuple-element.42), channel_id=1, source_target_pairs={{0,8},{4,12},{8,0},{12,4},{1,9},{5,13},{9,1},{13,5},{2,10},{6,14},... | collective-permute-start | bytes 393224 | tf_op jit(solution)/shard_map/ppermute | solution.py:529
  229.6 21.8 %copy-start.13 = (bf16[64,1024]{1,0:T(8,128)(2,1)}, bf16[64,1024]{1,0:T(8,128)(2,1)S(1)}, u32[]{:S(2)}) copy-start(bf16[64,1024]{1,0:T(8,128)(2,1)S(1)} %collective-permute-done.12.refs_1_) | copy-start | bytes 393220
  229.6 9.2 %collective-permute-start.14 = (bf16[64,1024]{1,0:T(8,128)(2,1)S(1)}, bf16[64,1024]{1,0:T(8,128)(2,1)S(1)}, u32[]{:S(2)}, u32[]{:S(2)}) collective-permute-start(bf16[64,1024]{1,0:T(8,128)(2,1)S(1)} %get-tuple-element.41), channel_id=1, source_target_pairs={{0,12},{4,8},{8,4},{12,0},{1,13},{5,9},{9,5},{13,1},{2,14},{6,10},... | collective-permute-start | bytes 393224 | tf_op jit(solution)/shard_map/ppermute | solution.py:529
  231.1 20.3 %copy-start.9 = (bf16[4,1,128,128]{3,2,1,0:T(8,128)(2,1)}, bf16[4,1,128,128]{3,2,1,0:T(8,128)(2,1)S(1)}, u32[]{:S(2)}) copy-start(bf16[4,1,128,128]{3,2,1,0:T(8,128)(2,1)S(1)} %pad_maximum_fusion.refs_5_) | copy-start | bytes 393220
  238.7 12.7 %copy-start.14 = (bf16[64,1024]{1,0:T(8,128)(2,1)}, bf16[64,1024]{1,0:T(8,128)(2,1)S(1)}, u32[]{:S(2)}) copy-start(bf16[64,1024]{1,0:T(8,128)(2,1)S(1)} %collective-permute-done.13.refs_2_) | copy-start | bytes 393220
  238.7 1.3 collective-permute-start.22
  238.7 8.7 %copy-start.15 = (bf16[64,1024]{1,0:T(8,128)(2,1)}, bf16[64,1024]{1,0:T(8,128)(2,1)S(1)}, u32[]{:S(2)}) copy-start(bf16[64,1024]{1,0:T(8,128)(2,1)S(1)} %collective-permute-done.14.refs_3_) | copy-start | bytes 393220
  238.7 6.4 %collective-permute-start.23 = (bf16[4,1,128,128]{3,2,1,0:T(8,128)(2,1)S(1)}, bf16[4,1,128,128]{3,2,1,0:T(8,128)(2,1)S(1)}, u32[]{:S(2)}, u32[]{:S(2)}) collective-permute-start(bf16[4,1,128,128]{3,2,1,0:T(8,128)(2,1)S(1)} %pad_maximum_fusion.refs_5_), channel_id=1, source_target_pairs={{0,2},{1,3},{2,0},{3,1},{4,6},{5,7},{6,4},{7,5},{8,10},{9,11},{10,... | collective-permute-start | bytes 393224 | tf_op jit(solution)/shard_map/ppermute | solution.py:529
  240.1 10.7 %copy-start.16 = (bf16[4,1,128,128]{3,2,1,0:T(8,128)(2,1)}, bf16[4,1,128,128]{3,2,1,0:T(8,128)(2,1)S(1)}, u32[]{:S(2)}) copy-start(bf16[4,1,128,128]{3,2,1,0:T(8,128)(2,1)S(1)} %collective-permute-done.22.refs_6_) | copy-start | bytes 393220
  240.1 7.4 %collective-permute-start.15 = (bf16[64,1024]{1,0:T(8,128)(2,1)S(1)}, bf16[64,1024]{1,0:T(8,128)(2,1)S(1)}, u32[]{:S(2)}, u32[]{:S(2)}) collective-permute-start(bf16[64,1024]{1,0:T(8,128)(2,1)S(1)} %fusion.2), channel_id=1, source_target_pairs={{0,2},{1,3},{2,0},{3,1},{4,6},{5,7},{6,4},{7,5},{8,10},{9,11},{10,... | collective-permute-start | bytes 393224 | tf_op jit(solution)/shard_map/ppermute | solution.py:529
  245.2 5.6 %copy-start.17 = (bf16[4,1,128,128]{3,2,1,0:T(8,128)(2,1)}, bf16[4,1,128,128]{3,2,1,0:T(8,128)(2,1)S(1)}, u32[]{:S(2)}) copy-start(bf16[4,1,128,128]{3,2,1,0:T(8,128)(2,1)S(1)} %collective-permute-done.23.refs_7_) | copy-start | bytes 393220
  245.2 5.5 %collective-permute-start.24 = (bf16[4,1,128,128]{3,2,1,0:T(8,128)(2,1)S(1)}, bf16[4,1,128,128]{3,2,1,0:T(8,128)(2,1)S(1)}, u32[]{:S(2)}, u32[]{:S(2)}) collective-permute-start(bf16[4,1,128,128]{3,2,1,0:T(8,128)(2,1)S(1)} %collective-permute-done.23.refs_7_), channel_id=1, source_target_pairs={{0,1},{1,0},{2,3},{3,2},{4,5},{5,4},{6,7},{7,6},{8,9},{9,8},{10,11... | collective-permute-start | bytes 393224 | tf_op jit(solution)/shard_map/ppermute | solution.py:529
  245.2 24.4 %copy-start.20 = (f32[1,256]{1,0:T(1,128)}, f32[1,256]{1,0:T(1,128)S(1)}, u32[]{:S(2)}) copy-start(f32[1,256]{1,0:T(1,128)S(1)} %fusion.7.refs_17_) | copy-start | bytes 3076
  247.4 3.3 %copy-start.18 = (bf16[64,1024]{1,0:T(8,128)(2,1)}, bf16[64,1024]{1,0:T(8,128)(2,1)S(1)}, u32[]{:S(2)}) copy-start(bf16[64,1024]{1,0:T(8,128)(2,1)S(1)} %collective-permute-done.15.refs_4_) | copy-start | bytes 393220
  247.4 9.5 %collective-permute-start.31 = (f32[1,256]{1,0:T(1,128)S(1)}, f32[1,256]{1,0:T(1,128)S(1)}, u32[]{:S(2)}, u32[]{:S(2)}) collective-permute-start(f32[1,256]{1,0:T(1,128)S(1)} %fusion.7.refs_17_), channel_id=1, source_target_pairs={{0,8},{4,12},{8,0},{12,4},{1,9},{5,13},{9,1},{13,5},{2,10},{6,14},... | collective-permute-start | bytes 3080 | tf_op jit(solution)/shard_map/ppermute | solution.py:529
  250.7 0.6 copy-start.19
  257.0 6.2 %collective-permute-start.25 = (bf16[64,1024]{1,0:T(8,128)(2,1)}, bf16[64,1024]{1,0:T(8,128)(2,1)S(1)}, u32[]{:S(2)}, u32[]{:S(2)}) collective-permute-start(bf16[64,1024]{1,0:T(8,128)(2,1)} %coefficients.1.refs_13_), channel_id=1, source_target_pairs={{0,4},{4,0},{8,12},{12,8},{1,5},{5,1},{9,13},{13,9},{2,6},{6,2},{1... | collective-permute-start | bytes 393224 | tf_op jit(solution)/shard_map/ppermute | solution.py:529
  257.0 12.6 %copy-start.22 = (f32[1,256]{1,0:T(1,128)}, f32[1,256]{1,0:T(1,128)S(1)}, u32[]{:S(2)}) copy-start(f32[1,256]{1,0:T(1,128)S(1)} %collective-permute-done.31.refs_18_) | copy-start | bytes 3076
  257.0 12.5 %collective-permute-start.26 = (bf16[64,1024]{1,0:T(8,128)(2,1)}, bf16[64,1024]{1,0:T(8,128)(2,1)S(1)}, u32[]{:S(2)}, u32[]{:S(2)}) collective-permute-start(bf16[64,1024]{1,0:T(8,128)(2,1)} %coefficients.1.refs_13_), channel_id=1, source_target_pairs={{0,8},{4,12},{8,0},{12,4},{1,9},{5,13},{9,1},{13,5},{2,10},{6,14},... | collective-permute-start | bytes 393224 | tf_op jit(solution)/shard_map/ppermute | solution.py:529
  258.0 11.6 %copy-start.8 = (bf16[256,2048]{1,0:T(8,128)(2,1)}, bf16[256,2048]{1,0:T(8,128)(2,1)S(1)}, u32[]{:S(2)}) copy-start(bf16[256,2048]{1,0:T(8,128)(2,1)S(1)} %collective-permute-done.1.refs_2_) | copy-start | bytes 3145732
  258.0 11.5 %collective-permute-start.27 = (bf16[64,1024]{1,0:T(8,128)(2,1)}, bf16[64,1024]{1,0:T(8,128)(2,1)S(1)}, u32[]{:S(2)}, u32[]{:S(2)}) collective-permute-start(bf16[64,1024]{1,0:T(8,128)(2,1)} %coefficients.1.refs_13_), channel_id=1, source_target_pairs={{0,12},{4,8},{8,4},{12,0},{1,13},{5,9},{9,5},{13,1},{2,14},{6,10},... | collective-permute-start | bytes 393224 | tf_op jit(solution)/shard_map/ppermute | solution.py:529
  263.1 6.4 %copy-start.10 = (bf16[64,1024]{1,0:T(8,128)(2,1)}, bf16[64,1024]{1,0:T(8,128)(2,1)S(1)}, u32[]{:S(2)}) copy-start(bf16[64,1024]{1,0:T(8,128)(2,1)S(1)} %collective-permute-done.25.refs_14_) | copy-start | bytes 393220
  269.5 0.7 copy-start.11
  269.5 0.7 copy-start.12
